TPU v7x, 256 devices: a whole 4x4x8 slice. The times are simulated.
256 devices in a mesh: dp: 8 (over y, core), seq: 32 (over z, x).
Axes of the slice: x: 4, y: 4, z: 8, core: 2. Of those that a mesh axis runs over, the one named last changes fastest.
Arguments:
- features: bfloat16 [8, 24576, 512], P('dp', 'seq'), may hold values from -12 to 12, as said below
- slot_kind: int32 [8, 96], P('dp', 'seq'), may hold values from 0 to 2, as said below
- block_gain: float32 [512], replicated, may hold values from 0.1 to 1.9
- block_shift: float32 [512], replicated, may hold values from -2 to 2
- block_weight: bfloat16 [4608, 512], replicated, may hold values from -0.09375 to 0.09375
- block_bias: float32 [512], replicated, may hold values from -2 to 2
- final_gain: float32 [512], replicated, may hold values from 0.1 to 1.9
- final_shift: float32 [512], replicated, may hold values from -2 to 2
- latent_weight: bfloat16 [512, 144], replicated, may hold values from -0.09375 to 0.09375
- latent_bias: float32 [16], replicated, may hold values from -2 to 2
- embed_weight: bfloat16 [64, 1152], P(None, 'dp'), may hold values from -0.75 to 0.75
- embed_bias: bfloat16 [1152], P('dp'), may hold values from -2 to 2
Outputs:
- sequence: bfloat16 [8, 4096, 1152], P('dp', 'seq')
Inputs may be any that keep to these rules, and one draw needn't show every extreme that they name: `slot_kind`: the live slots of a device (kind 1 or 2) come before its empty ones. In every dp group, the live slots of the devices with seq index below d number between 2 d and 2 d + 2, and 2 * 32 over the whole group; in every group some device has 3 live slots. `features`: finite values.
All inputs are finite; a program needn't handle non-finite values.
Results may differ from a plain program's by a relative error of at most 0.014.
Values may be sent and summed in bfloat16 or wider, within the bound.
A program may use at most 64 MiB of HBM per device.

v0:
```python
import jax
import jax.numpy as jnp
from jax import lax
from jax.sharding import PartitionSpec as P

GROUPS = 32
SLOT_ROWS = 32
SLOT_COLS = 8


LATENT_SHIFT = 0.0609
LATENT_SCALE = 1.5305
NORM_EPSILON = 1e-06
OFFSETS = [(-1, -1), (-1, 0), (-1, 1), (0, -1), (0, 0), (0, 1), (1, -1), (1, 0), (1, 1)]


def shifted(value, axis, steps):
    count = lax.axis_size(axis)
    leading, last = (max(0, -steps), min(count, count - steps))
    return lax.ppermute(value, axis, [(source, source + steps) for source in range(leading, last)])


def group_norm(values, slot_types, norm_gain, norm_shift):
    slot_count, height, across, channels = values.shape
    grouped = values.reshape(slot_count, 2, height // 2, across, GROUPS, channels // GROUPS)
    joined = (slot_types == 2)[:, None, None, None, None, None]
    half_centre = jnp.mean(grouped, axis=(2, 3, 5), keepdims=True)
    centre = jnp.where(joined, jnp.mean(half_centre, axis=1, keepdims=True), half_centre)
    centred = grouped - centre
    half_spread = jnp.mean(centred * centred, axis=(2, 3, 5), keepdims=True)
    spread = jnp.where(joined, jnp.mean(half_spread, axis=1, keepdims=True), half_spread)
    normed = (centred * lax.rsqrt(spread + NORM_EPSILON)).reshape(values.shape)
    return normed * norm_gain + norm_shift


def boundary_mask(slot_types, height, row_step, out_type):
    row_index = jnp.arange(height)
    edge_row = height // 2 if row_step < 0 else height // 2 - 1
    crossing = (slot_types == 1)[:, None] & (row_index == edge_row)[None, :]
    return jnp.where(crossing, 0.0, 1.0).astype(out_type)[:, :, None, None]


def neighbour(padded, slot_types, row_step, col_step):
    height = padded.shape[1] - 2
    across = padded.shape[2] - 2
    window = padded[
        :, 1 + row_step : 1 + row_step + height, 1 + col_step : 1 + col_step + across, :
    ]
    if row_step != 0:
        window = window * boundary_mask(slot_types, height, row_step, window.dtype)
    return window


def encode(
    slots,
    slot_types,
    block_gain,
    block_shift,
    block_weight,
    block_bias,
    final_gain,
    final_shift,
    latent_weight,
    latent_bias,
):
    slot_count, height, across, channels = slots.shape
    lat_width = latent_weight.shape[1] // 9
    first_act = jax.nn.silu(
        group_norm(slots.astype(jnp.float32), slot_types, block_gain, block_shift)
    ).astype(jnp.bfloat16)
    padded = jnp.pad(first_act, ((0, 0), (1, 1), (1, 1), (0, 0)))
    columns = jnp.concatenate(
        [neighbour(padded, slot_types, row_step, col_step) for row_step, col_step in OFFSETS],
        axis=-1,
    )
    conv_out = (
        jnp.dot(columns.reshape(-1, 9 * channels), block_weight, preferred_element_type=jnp.float32)
        + block_bias
    )
    inner = (
        (slots.reshape(-1, channels).astype(jnp.float32) + conv_out)
        .astype(jnp.bfloat16)
        .reshape(slots.shape)
    )
    second_act = jax.nn.silu(
        group_norm(inner.astype(jnp.float32), slot_types, final_gain, final_shift)
    ).astype(jnp.bfloat16)
    tap_terms = jnp.dot(
        second_act.reshape(-1, channels), latent_weight, preferred_element_type=jnp.float32
    )
    tap_terms = tap_terms.reshape(slot_count, height, across, 9 * lat_width)
    padded_terms = jnp.pad(tap_terms, ((0, 0), (1, 1), (1, 1), (0, 0)))
    latent = jnp.zeros((slot_count, height, across, lat_width), jnp.float32) + latent_bias
    for tap_number, (row_step, col_step) in enumerate(OFFSETS):
        piece_terms = padded_terms[..., tap_number * lat_width : (tap_number + 1) * lat_width]
        latent = latent + neighbour(piece_terms, slot_types, row_step, col_step)
    scaled = (latent - LATENT_SHIFT) * LATENT_SCALE
    patches = scaled.reshape(slot_count, height // 2, 2, across // 2, 2, lat_width).transpose(
        0, 1, 3, 2, 4, 5
    )
    return patches.reshape(slot_count * (height // 2) * (across // 2), 4 * lat_width).astype(
        jnp.bfloat16
    )


def local(
    features,
    slot_kind,
    block_gain,
    block_shift,
    block_weight,
    block_bias,
    final_gain,
    final_shift,
    latent_weight,
    latent_bias,
    embed_weight,
    embed_bias,
):
    seq_devices = lax.axis_size("seq")
    position = lax.axis_index("seq")
    slot_total = slot_kind.shape[1]
    channels = features.shape[2]
    all_types = lax.all_gather(slot_kind[0], "seq", axis=0, tiled=True)
    live_slots = (all_types.reshape(seq_devices, slot_total) > 0).astype(jnp.int32)
    counts = jnp.sum(live_slots, axis=1)
    starts = jnp.cumsum(counts) - counts
    embed_full, bias_full = (
        lax.all_gather(embed_weight, "dp", axis=1, tiled=True),
        lax.all_gather(embed_bias, "dp", axis=0, tiled=True),
    )
    own_slots = features[0].reshape(slot_total, SLOT_ROWS, SLOT_COLS, channels)
    carry_in = starts[position] - 2 * position
    slot_number = jnp.arange(2, dtype=jnp.int32)
    hid_width = embed_full.shape[1]
    patches = encode(
        own_slots,
        slot_kind[0],
        block_gain,
        block_shift,
        block_weight,
        block_bias,
        final_gain,
        final_shift,
        latent_weight,
        latent_bias,
    )
    tokens = (
        (
            jnp.dot(patches, embed_full, preferred_element_type=jnp.float32)
            + bias_full.astype(jnp.float32)
        )
        .astype(jnp.bfloat16)
        .reshape(slot_total, -1, hid_width)
    )
    padded = jnp.concatenate([tokens, jnp.zeros_like(tokens[:1])], axis=0)
    arrived = shifted(lax.dynamic_slice_in_dim(padded, 2 - carry_in, 2, 0), "seq", 1)
    kept = jnp.take(tokens, jnp.maximum(slot_number - carry_in, 0), axis=0)
    incoming = (slot_number < carry_in).reshape((2,) + (1,) * (tokens.ndim - 1))
    result = jnp.where(incoming, arrived, kept)
    return result.reshape(1, -1, hid_width)


def solution(mesh):
    in_specs = (
        P("dp", "seq", None),
        P("dp", "seq"),
        P(),
        P(),
        P(),
        P(),
        P(),
        P(),
        P(),
        P(),
        P(None, "dp"),
        P("dp"),
    )
    out_specs = P("dp", "seq", None)
    return jax.shard_map(local, mesh=mesh, in_specs=in_specs, out_specs=out_specs, check_vma=False)
```

profile of v0, /device:TPU:32, one launch (start us, length us, event | category | flops | bytes accessed | tf_op | source)
XLA Modules:
  0.0 126.7 jit_solution(9587615518974002790)
XLA Ops:
  0.0 8.2 %reshape.311 = f32[3,2,16,8,32,16]{5,4,3,2,1,0:T(8,128)} reshape(bf16[1,768,512]{2,1,0:T(8,128)(2,1)} %param.12) | data formatting | bytes 2359296 | tf_op jit(solution)/shard_map/convert_element_type | solution.py:69
  8.4 0.4 copy-done.12
  8.9 5.9 %reduce_sum.82 = f32[3,2,32]{2,1,0:T(2,128)S(1)} reduce(f32[3,2,16,8,32,16]{5,4,3,2,1,0:T(8,128)} %reshape.311, f32[]{:T(128)} %constant.57.clone.1), dimensions={2,3,5}, to_apply=%region_2.3 | reduce | flops 393024 | bytes 1573636 | tf_op jit(solution)/shard_map/reduce_sum | solution.py:27
  14.8 6.4 %multiply_reduce_fusion.1 = f32[3,2,32]{2,1,0:T(2,128)S(1)} fusion(f32[3,2,16,8,32,16]{5,4,3,2,1,0:T(8,128)} %reshape.311, f32[3,2,32]{2,1,0:T(2,128)S(1)} %broadcast_select_fusion.1), kind=kLoop, calls=%fused_computation.2 | loop fusion | flops 1179456 | bytes 1574400 | tf_op jit(solution)/shard_map/reduce_sum | solution.py:30
  21.4 0.3 mul.155
  21.6 1.1 mul.156
  23.0 1.7 %sub.72 = f32[3,32,512]{2,1,0:T(8,128)} reshape(f32[3,2,16,32,16]{4,3,2,1,0:T(8,128)S(1)} %sub.71) | data formatting | bytes 393216 | tf_op jit(solution)/shard_map/sub | solution.py:29
  24.8 1.6 %multiply_convert_fusion.1 = bf16[3,32,8,512]{3,2,1,0:T(8,128)(2,1)S(1)} fusion(f32[3,32,8,512]{3,2,1,0:T(8,128)S(1)} %bitcast.64, f32[512]{0:T(512)S(1)} %copy-done.5, f32[512]{0:T(512)S(1)} %copy-done.6, f32[3,32,512]{2,1,0:T(8,128)S(1)} %mul.156, f32[3,32,512]{2,1,0:T(8,128)} %sub.72), kind=kLoop, calls=%fused_computation.28 | loop fusion | flops 3538944 | bytes 2756608 | tf_op jit(solution)/shard_map/convert_element_type | solution.py:70
  27.4 0.5 copy-done.3
  27.8 0.5 constant_dynamic-update-slice_fusion
  28.5 0.3 fusion.14
  29.1 0.3 fusion.18
  29.3 0.6 copy-done.2
  29.9 3.8 %fusion.4 = f32[768,512]{1,0:T(8,128)S(1)} fusion(bf16[768,4608]{1,0:T(8,128)(2,1)S(1)} %bitcast.71, bf16[4608,512]{1,0:T(8,128)(2,1)S(1)} %bitcast.75, f32[512]{0:T(512)S(1)} %copy-done.10, bf16[1,768,512]{2,1,0:T(8,128)(2,1)S(1)} %copy-done.2), kind=kOutput, calls=%fused_computation.29 | convolution fusion | flops 3625844736 | bytes 14157824 | tf_op jit(solution)/shard_map/dot_general | solution.py:77
  33.7 6.9 %reshape.312 = f32[3,2,16,8,32,16]{5,4,3,2,1,0:T(8,128)} reshape(f32[768,512]{1,0:T(8,128)S(1)} %fusion.4) | data formatting | bytes 3145728 | tf_op jit(solution)/shard_map/convert_element_type | solution.py:86
  40.6 5.9 %reduce_sum.86 = f32[3,2,32]{2,1,0:T(2,128)S(1)} reduce(f32[3,2,16,8,32,16]{5,4,3,2,1,0:T(8,128)} %reshape.312, f32[]{:T(128)} %constant.57.clone.1), dimensions={2,3,5}, to_apply=%region_6.7 | reduce | flops 393024 | bytes 1573636 | tf_op jit(solution)/shard_map/reduce_sum | solution.py:27
  46.6 6.4 %multiply_reduce_fusion = f32[3,2,32]{2,1,0:T(2,128)S(1)} fusion(f32[3,2,16,8,32,16]{5,4,3,2,1,0:T(8,128)} %reshape.312, f32[3,2,32]{2,1,0:T(2,128)S(1)} %broadcast_select_fusion), kind=kLoop, calls=%fused_computation.1 | loop fusion | flops 1179456 | bytes 1574400 | tf_op jit(solution)/shard_map/reduce_sum | solution.py:30
  53.4 1.1 mul.172
  54.7 1.7 %sub.78 = f32[3,32,512]{2,1,0:T(8,128)} reshape(f32[3,2,16,32,16]{4,3,2,1,0:T(8,128)S(1)} %sub.77) | data formatting | bytes 393216 | tf_op jit(solution)/shard_map/sub | solution.py:29
  56.5 1.4 %multiply_convert_fusion = bf16[768,512]{1,0:T(8,128)(2,1)S(1)} fusion(f32[768,512]{1,0:T(8,128)S(1)} %fusion.4, f32[512]{0:T(512)S(1)} %copy-done.7, f32[512]{0:T(512)S(1)} %copy-done.8, f32[3,32,512]{2,1,0:T(8,128)S(1)} %mul.172, f32[3,32,512]{2,1,0:T(8,128)} %sub.78), kind=kLoop, calls=%fused_computation.27 | loop fusion | flops 3538944 | bytes 2756608 | tf_op jit(solution)/shard_map/convert_element_type | solution.py:87
  58.0 0.4 fusion.37
  58.4 1.0 fusion.36
  59.6 0.6 dynamic-slice.1
  61.2 14.9 %all-reduce.4 = bf16[1152]{0:T(1024)(128)(2,1)S(1)} all-reduce(bf16[1152]{0:T(1024)(128)(2,1)S(1)} %dynamic-update-slice.1), channel_id=1, replica_groups=mesh['dp'=8,'seq'=32] {'dp'}, use_global_device_ids=true, to_apply=%add.4 | all-reduce | flops 1152 | bytes 4608
  76.0 12.8 %all-gather.1 = bf16[8,144,64]{1,2,0:T(8,128)(2,1)S(1)} all-gather(bf16[1,144,64]{1,2,0:T(8,128)(2,1)S(1)} %bitcast.72), channel_id=1, replica_groups=mesh['dp'=8,'seq'=32] {'dp'}, dimensions={0}, use_global_device_ids=true | all-gather | bytes 165888 | tf_op jit(solution)/shard_map/all_gather | solution.py:129
  89.3 0.6 dynamic-slice
  90.6 22.4 %all-reduce.3 = s32[96]{0:T(128)S(1)} all-reduce(s32[96]{0:T(128)S(1)} %bitcast_dynamic-update-slice_fusion), channel_id=2, replica_groups=mesh['dp'=8,'seq'=32] {'seq'}, use_global_device_ids=true, to_apply=%add.3 | all-reduce | flops 96 | bytes 768
  113.6 0.6 dynamic_slice.6
  115.2 2.5 %collective-permute-start = (bf16[2,64,1152]{2,1,0:T(8,128)(2,1)S(1)}, bf16[2,64,1152]{2,1,0:T(8,128)(2,1)S(1)}, u32[]{:S(2)}, u32[]{:S(2)}) collective-permute-start(bf16[2,64,1152]{2,1,0:T(8,128)(2,1)S(1)} %pad_dynamic-slice_fusion), channel_id=1, source_target_pairs={{0,1},{1,2},{2,3},{3,4},{4,5},{5,6},{6,7},{7,8},{8,9},{9,10},{10,1... | collective-permute-start | bytes 884744 | tf_op jit(solution)/shard_map/ppermute | solution.py:20
  117.7 0.6 gather_fusion
  118.3 7.6 %collective-permute-done = bf16[2,64,1152]{2,1,0:T(8,128)(2,1)S(1)} collective-permute-done((bf16[2,64,1152]{2,1,0:T(8,128)(2,1)S(1)}, bf16[2,64,1152]{2,1,0:T(8,128)(2,1)S(1)}, u32[]{:S(2)}, u32[]{:S(2)}) %collective-permute-start) | collective-permute-done | bytes 294944 | tf_op jit(solution)/shard_map/ppermute | solution.py:20
  125.9 0.8 select_select_fusion
  (78 shorter events, 4.8 us)
Async XLA Ops:
  0.0 57.9 %copy-start = (bf16[512,144]{0,1:T(8,128)(2,1)S(1)}, bf16[512,144]{0,1:T(8,128)(2,1)}, u32[]{:S(2)}) copy-start(bf16[512,144]{0,1:T(8,128)(2,1)} %param.20) | copy-start | bytes 442372
  0.0 8.2 %copy-start.1 = (bf16[1,768,512]{2,1,0:T(8,128)(2,1)S(1)}, bf16[1,768,512]{2,1,0:T(8,128)(2,1)}, u32[]{:S(2)}) copy-start(bf16[1,768,512]{2,1,0:T(8,128)(2,1)} %param.12) | copy-start | bytes 2359300
  8.2 0.7 copy-start.12
  22.7 2.1 %copy-start.5 = (f32[512]{0:T(512)S(1)}, f32[512]{0:T(512)}, u32[]{:S(2)}) copy-start(f32[512]{0:T(512)} %param.15) | copy-start | bytes 6148
  22.7 2.1 %copy-start.6 = (f32[512]{0:T(512)S(1)}, f32[512]{0:T(512)}, u32[]{:S(2)}) copy-start(f32[512]{0:T(512)} %param.14) | copy-start | bytes 6148
  24.8 4.5 %slice-start = ((s8[4718592]{0:T(1024)(128)(4,1)}), s8[4194304]{0:T(1024)(128)(4,1)S(1)}, s32[]{:S(2)}) async-start(s8[4718592]{0:T(1024)(128)(4,1)} %bitcast.74), calls=%async_computation | async-start | bytes 8388608
  26.9 0.9 copy-start.3
  27.8 1.5 %slice-start.1 = ((s8[4718592]{0:T(1024)(128)(4,1)}), s8[524288]{0:T(1024)(128)(4,1)S(1)}, s32[]{:S(2)}) async-start(s8[4718592]{0:T(1024)(128)(4,1)} %bitcast.74), calls=%async_computation.1 | async-start | bytes 1048576
  28.8 1.1 copy-start.2
  28.8 1.1 copy-start.10
  54.4 2.0 %copy-start.7 = (f32[512]{0:T(512)S(1)}, f32[512]{0:T(512)}, u32[]{:S(2)}) copy-start(f32[512]{0:T(512)} %param.19) | copy-start | bytes 6148
  54.4 2.0 %copy-start.8 = (f32[512]{0:T(512)S(1)}, f32[512]{0:T(512)}, u32[]{:S(2)}) copy-start(f32[512]{0:T(512)} %param.18) | copy-start | bytes 6148
  56.5 1.9 %copy-start.9 = (f32[16]{0:T(128)S(1)}, f32[16]{0:T(128)}, u32[]{:S(2)}) copy-start(f32[16]{0:T(128)} %param.21) | copy-start | bytes 196
  57.9 1.7 %copy-start.14 = (u32[256]{0:T(256)S(1)}, u32[256]{0:T(256)}, u32[]{:S(2)}) copy-start(u32[256]{0:T(256)} %constant.85) | copy-start | bytes 3076
  57.9 3.0 %copy-start.11 = (bf16[144]{0:T(256)(128)(2,1)S(1)}, bf16[144]{0:T(256)(128)(2,1)}, u32[]{:S(2)}) copy-start(bf16[144]{0:T(256)(128)(2,1)} %param.23) | copy-start | bytes 868
  57.9 18.1 %copy-start.4 = (bf16[64,144]{1,0:T(8,128)(2,1)S(1)}, bf16[64,144]{1,0:T(8,128)(2,1)}, u32[]{:S(2)}) copy-start(bf16[64,144]{1,0:T(8,128)(2,1)} %param.22) | copy-start | bytes 55300
  58.3 30.9 %copy-start.13 = (u32[256]{0:T(256)S(1)}, u32[256]{0:T(256)}, u32[]{:S(2)}) copy-start(u32[256]{0:T(256)} %constant.80) | copy-start | bytes 3076
  115.2 10.7 %collective-permute-start = (bf16[2,64,1152]{2,1,0:T(8,128)(2,1)S(1)}, bf16[2,64,1152]{2,1,0:T(8,128)(2,1)S(1)}, u32[]{:S(2)}, u32[]{:S(2)}) collective-permute-start(bf16[2,64,1152]{2,1,0:T(8,128)(2,1)S(1)} %pad_dynamic-slice_fusion), channel_id=1, source_target_pairs={{0,1},{1,2},{2,3},{3,4},{4,5},{5,6},{6,7},{7,8},{8,9},{9,10},{10,1... | collective-permute-start | bytes 884744 | tf_op jit(solution)/shard_map/ppermute | solution.py:20
where the time goes:
time: 127 us
  blocking collectives  50.1 us (39%)
  other arithmetic  32.4 us (26%)
  local copies, waits for them, and re-layouts  27.3 us (21%)
  waiting for transfers between devices  7.57 us (6%)
  matrix products  4.42 us (3%)
  starting transfers between devices  2.51 us (2%)
  between operations  2.4 us (2%)
    unnamed x2, blocking collectives  37.3 us
    all_gather x1, blocking collectives, local(): lax.all_gather(embed_weight, 'dp', axis=1, tiled=True)  12.8 us
    reduce_sum x2, other arithmetic, group_norm(): half_spread = jnp.mean(centred * centred, axis=(2, 3, 5), keepdims=True)  12.8 us
    reduce_sum x2, other arithmetic, group_norm(): half_centre = jnp.mean(grouped, axis=(2, 3, 5), keepdims=True)  11.7 us
    convert_element_type x1, local copies, waits for them, and re-layouts, encode(): slots.astype(jnp.float32)  8.2 us
    ppermute x1, waiting for transfers between devices, shifted(): lax.ppermute(value, axis, [(source, source + steps) for source in range(l...  7.57 us
    convert_element_type x1, local copies, waits for them, and re-layouts, encode(): inner.astype(jnp.float32)  6.89 us
    sub x4, local copies, waits for them, and re-layouts, group_norm(): centred = grouped - centre  3.99 us
  transfers between devices with their start and end apart: 1, of which 1 were waited for; matrix products, arithmetic and copies ran while one was open for 0% of the time, Pallas kernels for 0%

commit v1 on v0

v1 whole, which is shorter than its diff:
```python
import functools
import jax
import jax.numpy as jnp
from jax import lax
from jax.experimental import pallas as pl
from jax.experimental.pallas import tpu as pltpu
from jax.sharding import PartitionSpec as P

F32, BF16, I32 = jnp.float32, jnp.bfloat16, jnp.int32
MESH = pl.DeviceIdType.MESH
LATENT_SHIFT = 0.0609
LATENT_SCALE = 1.5305
EPS = 1e-06
C = 512
TAPS = [(a, b) for a in (-1, 0, 1) for b in (-1, 0, 1)]


def iota(shape, dim):
    return lax.broadcasted_iota(I32, shape, dim)


def lane_tiles(v):
    return [v[:, 128 * i : 128 * i + 128] for i in range(v.shape[1] // 128)]


def group_sums(parts, block):
    rows = jnp.concatenate([t for p in parts for t in lane_tiles(p)], axis=0)
    hi = rows.astype(BF16)
    rest = rows - hi.astype(F32)
    mid = rest.astype(BF16)
    low = (rest - mid.astype(F32)).astype(BF16)
    sums = jnp.dot(jnp.concatenate([hi, mid, low], axis=0), block, preferred_element_type=F32)
    count = rows.shape[0]
    total = sums[:count] + sums[count : 2 * count] + sums[2 * count :]
    out = []
    for i in range(len(parts)):
        tiles = []
        for j in range(4):
            tile = total[32 * i + 8 * j : 32 * i + 8 * j + 8]
            tiles.append(jnp.broadcast_to(jnp.sum(tile, axis=0, keepdims=True), (8, 128)))
        out.append(jnp.concatenate(tiles, axis=1))
    return out


def norm_scales(load, block, joined, gain, shift):
    zero = jnp.zeros((8, C), F32)
    low, high = zero, zero
    for r in range(16):
        x0, x1 = load(r)
        low, high = low + x0, high + x1
    m0, m1 = group_sums([low, high], block)
    m0, m1 = m0 * (1.0 / 2048), m1 * (1.0 / 2048)
    both = (m0 + m1) * 0.5
    c0, c1 = jnp.where(joined, both, m0), jnp.where(joined, both, m1)
    low, high = zero, zero
    for r in range(16):
        x0, x1 = load(r)
        x0, x1 = x0 - c0, x1 - c1
        low, high = low + x0 * x0, high + x1 * x1
    v0, v1 = group_sums([low, high], block)
    v0, v1 = v0 * (1.0 / 2048), v1 * (1.0 / 2048)
    both = (v0 + v1) * 0.5
    v0, v1 = jnp.where(joined, both, v0), jnp.where(joined, both, v1)
    s0 = lax.rsqrt(v0 + EPS) * gain * 0.5
    s1 = lax.rsqrt(v1 + EPS) * gain * 0.5
    return c0, c1, s0, s1, jnp.broadcast_to(shift * 0.5, (8, C))


def silu_half(half):
    return half + half * jnp.tanh(half)


def side_shifts(y):
    col = iota((8, C), 0)
    left = jnp.where(col >= 1, pltpu.roll(y, 1, 0), 0.0)
    right = jnp.where(col <= 6, pltpu.roll(y, 7, 0), 0.0)
    return left, y, right


def pair(top, bottom):
    return jnp.concatenate([top, bottom], axis=0).astype(BF16)


def norm_first(load, block, joined, gain, shift, pad):
    c0, c1, s0, s1, t = norm_scales(load, block, joined, gain, shift)
    zero = jnp.zeros((8, C), F32)
    for r in range(16):
        x0, x1 = load(r)
        y0, y1 = silu_half((x0 - c0) * s0 + t), silu_half((x1 - c1) * s1 + t)
        sides0, sides1 = side_shifts(y0), side_shifts(y1)
        for b in range(3):
            pad[b, 16 * (r + 1) : 16 * (r + 2), :] = pair(sides0[b], sides1[b])
            if r == 0:
                pad[b, 16 * 17 : 16 * 18, :] = pair(jnp.where(joined, sides1[b], 0.0), zero)
            if r == 15:
                pad[b, 0:16, :] = pair(zero, jnp.where(joined, sides0[b], 0.0))


def conv(pad, w_ref):
    lhs = jnp.concatenate(
        [pad[b + 1, 16 * (a + 1) : 16 * (a + 1) + 256, :] for a, b in TAPS], axis=1
    )
    return jnp.dot(lhs, w_ref[...], preferred_element_type=F32)


def norm_second(load, block, joined, gain, shift, act):
    c0, c1, s0, s1, t = norm_scales(load, block, joined, gain, shift)
    for r in range(16):
        x0, x1 = load(r)
        act[16 * r : 16 * r + 16, :] = pair(
            silu_half((x0 - c0) * s0 + t), silu_half((x1 - c1) * s1 + t)
        )


def latent_patches(act, lw3, lat_bias, joined, select):
    terms = jnp.dot(act[...], lw3, preferred_element_type=F32)
    joined = joined[:, :128]
    zero = jnp.zeros((8, 128), F32)

    def part(a, r, h):
        return terms[16 * r + 8 * h : 16 * r + 8 * h + 8, 128 * (a + 1) : 128 * (a + 2)]

    col = iota((8, 128), 0)
    lane = iota((8, 128), 1)
    rows = []
    for p in range(8):
        for h in range(2):
            total = None
            for i in range(2):
                r = 2 * p + i
                above = part(-1, r - 1, h) if r > 0 else (jnp.where(joined, part(-1, 15, 0), 0.0) if h == 1 else zero)
                below = part(1, r + 1, h) if r < 15 else (jnp.where(joined, part(1, 0, 1), 0.0) if h == 0 else zero)
                z = above + part(0, r, h) + below
                left = jnp.where(col >= 1, pltpu.roll(z, 1, 0), 0.0)
                right = jnp.where(col <= 6, pltpu.roll(z, 7, 0), 0.0)
                if i == 0:
                    lat = left + pltpu.roll(z, 96, 1) + pltpu.roll(right, 64, 1)
                else:
                    lat = pltpu.roll(left, 32, 1) + z + pltpu.roll(right, 96, 1)
                lat = (lat + lat_bias - LATENT_SHIFT) * LATENT_SCALE
                own = (lane // 16) == (2 * i + col % 2)
                lat = jnp.where(own, lat, 0.0)
                total = lat if total is None else total + lat
            rows.append(total)
    cells = jnp.concatenate(rows, axis=0).astype(BF16)
    return jnp.dot(select, cells, preferred_element_type=F32).astype(BF16)


def constants(lw, lat_bias):
    block = jnp.where(iota((128, 128), 0) // 16 == iota((128, 128), 1) // 16, 1.0, 0.0).astype(BF16)
    k, n = iota((144, 384), 0), iota((144, 384), 1)
    group = (n % 128) // 16
    source = ((n // 128) * 3 + group // 2) * 16 + n % 16
    place = jnp.where((k == source) & (group < 6), 1.0, 0.0).astype(BF16)
    lw3 = jnp.dot(lw, place, preferred_element_type=F32).astype(BF16)
    t, m = iota((64, 128), 0), iota((64, 128), 1)
    same = (m // 16 == (t // 4) % 8) & ((m // 8) % 2 == t // 32) & ((m % 8) // 2 == t % 4)
    select = jnp.where(same, 1.0, 0.0).astype(BF16)
    return block, lw3, select


N_SEQ = 32
N_DP = 8


def kernel(
    kind, feat_hbm, bg, bs, w_hbm, bb, fg, fs, lw, lb, ew, eb, out,
    feat, slots, w, pad, inner, act, lanes, mine, counts, shard, shards, full, sent, got,
    feat_sem, w_sem, count_send, count_recv, shard_send, shard_recv, patch_send, patch_recv,
):
    seat, row = lax.axis_index("seq"), lax.axis_index("dp")
    ahead = lax.rem(seat + 1, N_SEQ)
    feat_copy = pltpu.make_async_copy(feat_hbm.at[0], feat, feat_sem)
    feat_copy.start()
    w_copy = pltpu.make_async_copy(w_hbm, w, w_sem)
    w_copy.start()

    barrier = pltpu.get_barrier_semaphore()

    def greet_seq(i, carry):
        pl.semaphore_signal(barrier, inc=1, device_id={"seq": lax.rem(seat + i, N_SEQ)}, device_id_type=MESH)
        return carry

    def greet_dp(i, carry):
        pl.semaphore_signal(barrier, inc=1, device_id={"dp": lax.rem(row + i, N_DP)}, device_id_type=MESH)
        return carry

    lax.fori_loop(1, N_SEQ, greet_seq, 0)
    lax.fori_loop(1, N_DP, greet_dp, 0)

    live = [(kind[0, i] > 0).astype(I32) for i in range(3)]
    n = live[0] + live[1] + live[2]
    kinds = [
        jnp.where(n == 3, kind[0, 2], jnp.where(n == 2, kind[0, 1], kind[0, 0])),
        jnp.where(n == 2, kind[0, 0], kind[0, 1]),
        jnp.where(n == 3, kind[0, 0], kind[0, 2]),
    ]
    mine[...] = jnp.full((1, 128), n, I32)
    counts[pl.ds(seat, 1)] = jnp.full((1, 1, 128), n, I32)
    shard[0:64, :] = ew[...]
    shard[64:80, :] = jnp.broadcast_to(eb[...], (16, 144))
    shards[pl.ds(row, 1)] = shard[...].reshape(1, 80, 144)
    lanes[...] = jnp.zeros((8, 128), F32)
    lanes[0:1, 0:16] = lb[...]
    lat_bias = lanes[...]
    for step in (16, 32, 64):
        lat_bias = lat_bias + pltpu.roll(lat_bias, step, 1)
    lat_bias = lat_bias[0:1]
    block, lw3, select = constants(lw[...], lat_bias)

    def count_copy(i):
        return pltpu.make_async_remote_copy(
            src_ref=mine,
            dst_ref=counts.at[seat],
            send_sem=count_send.at[i],
            recv_sem=count_recv.at[i],
            device_id={"seq": lax.rem(seat + i, N_SEQ)},
            device_id_type=MESH,
        )

    def shard_copy(i):
        return pltpu.make_async_remote_copy(
            src_ref=shard,
            dst_ref=shards.at[row],
            send_sem=shard_send.at[i],
            recv_sem=shard_recv.at[i],
            device_id={"dp": lax.rem(row + i, N_DP)},
            device_id_type=MESH,
        )

    def patch_copy(t):
        return pltpu.make_async_remote_copy(
            src_ref=sent.at[t],
            dst_ref=got.at[t],
            send_sem=patch_send.at[t],
            recv_sem=patch_recv.at[t],
            device_id={"seq": ahead},
            device_id_type=MESH,
        )

    number = jnp.full((16, C), n, I32)
    feat_copy.wait()
    for i in range(16):
        first, middle, last = [feat[256 * k + 16 * i : 256 * k + 16 * i + 16, :] for k in range(3)]
        part = slice(16 * i, 16 * i + 16)
        slots[0, part, :] = jnp.where(number == 3, last, jnp.where(number == 2, middle, first))
        slots[1, part, :] = jnp.where(number == 2, first, middle)
        slots[2, part, :] = jnp.where(number == 3, first, last)
    for t in range(3):
        joined = jnp.full((8, C), kinds[t], I32) == 2

        def load(r):
            return slots[t, 8 * r : 8 * r + 8, :].astype(F32), slots[t, 128 + 8 * r : 136 + 8 * r, :].astype(F32)

        norm_first(load, block, joined, bg[...], bs[...], pad)
        if t == 0:
            w_copy.wait()
        res = conv(pad, w)
        bias = jnp.broadcast_to(bb[...], (8, C))
        for r in range(16):
            x0, x1 = load(r)
            top, bottom = res[16 * r : 16 * r + 8], res[16 * r + 8 : 16 * r + 16]
            inner[16 * r : 16 * r + 16, :] = pair(top + x0 + bias, bottom + x1 + bias)

        if t == 0:
            pl.semaphore_wait(barrier, N_SEQ + N_DP - 2)

            def send_count(i, carry):
                count_copy(i).start()
                return carry

            def send_shard(i, carry):
                shard_copy(i).start()
                return carry

            lax.fori_loop(1, N_SEQ, send_count, 0)
            lax.fori_loop(1, N_DP, send_shard, 0)

        def load_inner(r):
            v = inner[16 * r : 16 * r + 16, :].astype(F32)
            return v[:8], v[8:]

        norm_second(load_inner, block, joined, fg[...], fs[...], act)
        sent[t] = latent_patches(act, lw3, lat_bias, joined, select)
        if t < 2:
            patch_copy(t).start()

    def wait_count(i, carry):
        count_copy(i).wait()
        return carry

    def wait_shard(i, carry):
        shard_copy(i).wait()
        return carry

    lax.fori_loop(1, N_SEQ, wait_count, 0)
    lax.fori_loop(1, N_DP, wait_shard, 0)
    for i in range(N_DP):
        full[:, 144 * i : 144 * i + 144] = shards[i]
    before = iota((N_SEQ, 1, 128), 0) < seat
    carry_in = jnp.sum(jnp.where(before, counts[...], 0), axis=0) - 2 * seat
    for t in range(2):
        patch_copy(t).wait()

    def wide(v):
        return jnp.broadcast_to(v, (64, 128))

    carry_in = wide(carry_in)
    number = wide(jnp.full((1, 128), n, I32))
    own = [sent[t].astype(F32) for t in range(3)]
    came = [got[t].astype(F32) for t in range(2)]
    newest = jnp.where(number == 3, own[2], jnp.where(number == 2, own[1], own[0]))
    second = jnp.where(number == 3, own[1], own[0])
    out0 = jnp.where(carry_in == 0, newest, jnp.where(carry_in == 1, came[0], came[1]))
    out1 = jnp.where(carry_in == 0, second, jnp.where(carry_in == 1, newest, came[0]))
    patches = jnp.concatenate([out0, out1], axis=0).astype(BF16)[:, :64]
    tokens = jnp.dot(patches, full[0:64, :], preferred_element_type=F32)
    out[0] = (tokens + full[64:65, :].astype(F32)).astype(BF16)


def local(feat, kind, bg, bs, w, bb, fg, fs, lw, lb, ew, eb):
    in_vmem = pl.BlockSpec(memory_space=pltpu.VMEM)
    in_hbm = pl.BlockSpec(memory_space=pl.ANY)
    in_smem = pl.BlockSpec(memory_space=pltpu.SMEM)
    dma = pltpu.SemaphoreType.DMA
    return pl.pallas_call(
        kernel,
        out_shape=jax.ShapeDtypeStruct((1, 128, 1152), BF16),
        in_specs=[in_smem, in_hbm, in_vmem, in_vmem, in_hbm] + [in_vmem] * 7,
        out_specs=in_vmem,
        scratch_shapes=[
            pltpu.VMEM((768, C), BF16),
            pltpu.VMEM((3, 256, C), BF16),
            pltpu.VMEM((9 * C, C), BF16),
            pltpu.VMEM((3, 288, C), BF16),
            pltpu.VMEM((256, C), BF16),
            pltpu.VMEM((256, C), BF16),
            pltpu.VMEM((8, 128), F32),
            pltpu.VMEM((1, 128), I32),
            pltpu.VMEM((N_SEQ, 1, 128), I32),
            pltpu.VMEM((80, 144), BF16),
            pltpu.VMEM((N_DP, 80, 144), BF16),
            pltpu.VMEM((80, 1152), BF16),
            pltpu.VMEM((3, 64, 128), BF16),
            pltpu.VMEM((2, 64, 128), BF16),
            dma,
            dma,
            dma((N_SEQ,)),
            dma((N_SEQ,)),
            dma((N_DP,)),
            dma((N_DP,)),
            dma((2,)),
            dma((2,)),
        ],
        compiler_params=pltpu.CompilerParams(
            collective_id=0, has_side_effects=True, vmem_limit_bytes=60 << 20
        ),
    )(
        kind, feat, bg.reshape(1, C), bs.reshape(1, C), w, bb.reshape(1, C), fg.reshape(1, C),
        fs.reshape(1, C), lw, lb.reshape(1, 16), ew, eb.reshape(1, 144),
    )


def solution(mesh):
    shared = P()
    return jax.shard_map(
        local,
        mesh=mesh,
        in_specs=(P("dp", "seq", None), P("dp", "seq")) + (shared,) * 8 + (P(None, "dp"), P("dp")),
        out_specs=P("dp", "seq", None),
        check_vma=False,
    )
```

time: 127 us -> 25.7 us (0.20)
  the two profiles are of different devices: /device:TPU:32 before, /device:TPU:1 now
where the time goes in v1:
time: 25.7 us; the launch traced here: 25.5 us
  Pallas kernels  20.8 us (81%)
  local copies, waits for them, and re-layouts  4.68 us (18%)
    pallas_call x1, Pallas kernels, local(): pl.pallas_call(kernel, out_shape=jax.ShapeDtypeStruct((1, 128, 1152), BF1...  20.8 us
    unnamed x2, local copies, waits for them, and re-layouts  3.45 us
    reshape x1, local copies, waits for them, and re-layouts, local(): eb.reshape(1, 144)  1.23 us

profile of v1, /device:TPU:1, one launch (start us, length us, event | category | flops | bytes accessed | tf_op | source)
XLA Modules:
  0.0 25.5 jit_solution(13933207085858861552)
XLA Ops:
  0.0 1.2 %reshape.27.eb = bf16[1,144]{1,0:T(2,128)(2,1)} reshape(bf16[144]{0:T(256)(128)(2,1)} %param.23) | data formatting | bytes 576 | tf_op jit(solution)/shard_map/reshape | solution.py:360
  1.2 1.7 %copy.13.lw = bf16[512,144]{1,0:T(8,128)(2,1)} copy(bf16[512,144]{0,1:T(8,128)(2,1)} %param.20) | data formatting | bytes 294912 | tf_op args[8]
  3.0 20.8 %shard_map.118 = bf16[1,128,1152]{2,1,0:T(8,128)(2,1)} custom-call(s32[1,3]{1,0:T(1,128)} %kind.1, bf16[1,768,512]{2,1,0:T(8,128)(2,1)} %feat_hbm.1, f32[1,512]{1,0:T(1,128)} %bitcast.6, f32[1,512]{1,0:T(1,128)} %bitcast.7, bf16[4608,512]{1,0:T(8,128)(2,1)} %w_hbm.1, f32[1,512]{1,0:T(1,128)} %bitcast.8, f32[1,512]{1,0:T(1,128)} %bitcast.9, ...), custom_call_target="tpu_custom_call" | custom-call | tf_op jit(solution)/shard_map/pallas_call | solution.py:326
  23.8 1.7 %copy.15 = bf16[1,128,1152]{2,1,0:T(8,128)(2,1)} copy(bf16[1,128,1152]{2,1,0:T(8,128)(2,1)} %shard_map.118) | data formatting | bytes 589824

commit v2 on v1

v2 whole, which is shorter than its diff:
```python
import functools
import jax
import jax.numpy as jnp
from jax import lax
from jax.experimental import pallas as pl
from jax.experimental.pallas import tpu as pltpu
from jax.sharding import PartitionSpec as P

F32, BF16, I32 = jnp.float32, jnp.bfloat16, jnp.int32
MESH = pl.DeviceIdType.MESH
LATENT_SHIFT = 0.0609
LATENT_SCALE = 1.5305
EPS = 1e-06
C = 512
HID = 1152
TAPS = [(a, b) for a in (-1, 0, 1) for b in (-1, 0, 1)]
N_DP, N_Z, N_X = 8, 8, 4


def iota(shape, dim):
    return lax.broadcasted_iota(I32, shape, dim)


def lane_tiles(v):
    return [v[:, 128 * i : 128 * i + 128] for i in range(v.shape[1] // 128)]


def group_sums(parts, block):
    rows = jnp.concatenate([t for p in parts for t in lane_tiles(p)], axis=0)
    hi = rows.astype(BF16)
    rest = rows - hi.astype(F32)
    mid = rest.astype(BF16)
    low = (rest - mid.astype(F32)).astype(BF16)
    sums = jnp.dot(jnp.concatenate([hi, mid, low], axis=0), block, preferred_element_type=F32)
    count = rows.shape[0]
    total = sums[:count] + sums[count : 2 * count] + sums[2 * count :]
    out = []
    for i in range(len(parts)):
        tiles = []
        for j in range(4):
            tile = total[32 * i + 8 * j : 32 * i + 8 * j + 8]
            tiles.append(jnp.broadcast_to(jnp.sum(tile, axis=0, keepdims=True), (8, 128)))
        out.append(jnp.concatenate(tiles, axis=1))
    return out


def norm_scales(load, block, joined, gain, shift):
    zero = jnp.zeros((8, C), F32)
    low, high = zero, zero
    for r in range(16):
        x0, x1 = load(r)
        low, high = low + x0, high + x1
    m0, m1 = group_sums([low, high], block)
    m0, m1 = m0 * (1.0 / 2048), m1 * (1.0 / 2048)
    both = (m0 + m1) * 0.5
    c0, c1 = jnp.where(joined, both, m0), jnp.where(joined, both, m1)
    low, high = zero, zero
    for r in range(16):
        x0, x1 = load(r)
        x0, x1 = x0 - c0, x1 - c1
        low, high = low + x0 * x0, high + x1 * x1
    v0, v1 = group_sums([low, high], block)
    v0, v1 = v0 * (1.0 / 2048), v1 * (1.0 / 2048)
    both = (v0 + v1) * 0.5
    v0, v1 = jnp.where(joined, both, v0), jnp.where(joined, both, v1)
    s0 = lax.rsqrt(v0 + EPS) * gain * 0.5
    s1 = lax.rsqrt(v1 + EPS) * gain * 0.5
    return c0, c1, s0, s1, jnp.broadcast_to(shift * 0.5, (8, C))


def silu_half(half):
    return half + half * jnp.tanh(half)


def side_shifts(y):
    col = iota((8, C), 0)
    left = jnp.where(col >= 1, pltpu.roll(y, 1, 0), 0.0)
    right = jnp.where(col <= 6, pltpu.roll(y, 7, 0), 0.0)
    return left, y, right


def pair(top, bottom):
    return jnp.concatenate([top, bottom], axis=0).astype(BF16)


def norm_first(load, block, joined, gain, shift, pad):
    c0, c1, s0, s1, t = norm_scales(load, block, joined, gain, shift)
    zero = jnp.zeros((8, C), F32)
    for r in range(16):
        x0, x1 = load(r)
        y0, y1 = silu_half((x0 - c0) * s0 + t), silu_half((x1 - c1) * s1 + t)
        sides0, sides1 = side_shifts(y0), side_shifts(y1)
        for b in range(3):
            pad[b, 16 * (r + 1) : 16 * (r + 2), :] = pair(sides0[b], sides1[b])
            if r == 0:
                pad[b, 16 * 17 : 16 * 18, :] = pair(jnp.where(joined, sides1[b], 0.0), zero)
            if r == 15:
                pad[b, 0:16, :] = pair(zero, jnp.where(joined, sides0[b], 0.0))


def conv(pad, w, res):
    lhs = jnp.concatenate(
        [pad[b + 1, 16 * (a + 1) : 16 * (a + 1) + 256, :] for a, b in TAPS], axis=1
    )
    res[...] = jnp.dot(lhs, w[...], preferred_element_type=F32)


def residual(load, res, bias, inner):
    for r in range(16):
        x0, x1 = load(r)
        top, bottom = res[16 * r : 16 * r + 8, :], res[16 * r + 8 : 16 * r + 16, :]
        inner[16 * r : 16 * r + 16, :] = pair(top + x0 + bias, bottom + x1 + bias)


def norm_second(load, block, joined, gain, shift, act):
    c0, c1, s0, s1, t = norm_scales(load, block, joined, gain, shift)
    for r in range(16):
        x0, x1 = load(r)
        act[16 * r : 16 * r + 16, :] = pair(
            silu_half((x0 - c0) * s0 + t), silu_half((x1 - c1) * s1 + t)
        )


def latent_patches(act, lw3, lat_bias, joined, select):
    terms = jnp.dot(act[...], lw3, preferred_element_type=F32)
    joined = joined[:, :128]
    zero = jnp.zeros((8, 128), F32)

    def part(a, r, h):
        return terms[16 * r + 8 * h : 16 * r + 8 * h + 8, 128 * (a + 1) : 128 * (a + 2)]

    col = iota((8, 128), 0)
    lane = iota((8, 128), 1)
    rows = []
    for p in range(8):
        for h in range(2):
            total = None
            for i in range(2):
                r = 2 * p + i
                above = part(-1, r - 1, h) if r > 0 else (jnp.where(joined, part(-1, 15, 0), 0.0) if h == 1 else zero)
                below = part(1, r + 1, h) if r < 15 else (jnp.where(joined, part(1, 0, 1), 0.0) if h == 0 else zero)
                z = above + part(0, r, h) + below
                left = jnp.where(col >= 1, pltpu.roll(z, 1, 0), 0.0)
                right = jnp.where(col <= 6, pltpu.roll(z, 7, 0), 0.0)
                if i == 0:
                    lat = left + pltpu.roll(z, 96, 1) + pltpu.roll(right, 64, 1)
                else:
                    lat = pltpu.roll(left, 32, 1) + z + pltpu.roll(right, 96, 1)
                lat = (lat + lat_bias - LATENT_SHIFT) * LATENT_SCALE
                own = (lane // 16) == (2 * i + col % 2)
                lat = jnp.where(own, lat, 0.0)
                total = lat if total is None else total + lat
            rows.append(total)
    cells = jnp.concatenate(rows, axis=0).astype(BF16)
    return jnp.dot(select, cells, preferred_element_type=F32).astype(BF16)


def tap_columns(lwt, lw3):
    zero = jnp.zeros((16, C), BF16)
    for a in range(3):
        taps = [lwt[16 * (3 * a + b) : 16 * (3 * a + b) + 16, :] for b in range(3)]
        rows = jnp.concatenate([taps[0], taps[0], taps[1], taps[1], taps[2], taps[2], zero, zero], axis=0)
        lw3[:, 128 * a : 128 * a + 128] = rows.T


def masks():
    block = jnp.where(iota((128, 128), 0) // 16 == iota((128, 128), 1) // 16, 1.0, 0.0).astype(BF16)
    t, m = iota((64, 128), 0), iota((64, 128), 1)
    same = (m // 16 == (t // 4) % 8) & ((m // 8) % 2 == t // 32) & ((m % 8) // 2 == t % 4)
    return block, jnp.where(same, 1.0, 0.0).astype(BF16)


DP_ORDER = (6, 4, 2, 7, 5, 3, 1, 0)


def exchange(pairs, start_now):
    for condition, copy, ready in pairs:

        @pl.when(condition)
        def _(copy=copy, ready=ready):
            if not start_now:
                pl.semaphore_wait(ready, 1)
            copy.start()


def kernel(
    kind_hbm, feat_hbm, bg_hbm, bs_hbm, w_hbm, bb_hbm, fg_hbm, fs_hbm, lw_hbm, lb_hbm, ew_hbm, eb_hbm,
    patch_out, embed_out,
    kind, feat, bg, bs, w, bb, fg, fs, lw, lb, ew, eb,
    slots, pad, res, inner, act, lw3, lanes, mine, rowsum, xcounts, zsums, shard, shards, sent, got,
    in_sem, x_send, x_recv, z_send, z_recv, d_send, d_recv, p_send, p_recv, x_ready, z_ready, d_ready,
):
    seat, row = lax.axis_index("seq"), lax.axis_index("dp")
    z, x = seat // N_X, lax.rem(seat, N_X)
    rank = jnp.where(row == 0, 7, jnp.where(lax.rem(row, 2) == 0, 3 - row // 2, 6 - row // 2))

    def at_x(i):
        return {"seq": z * N_X + i}

    def at_z(i):
        return {"seq": i * N_X + x}

    fetches = [
        pltpu.make_async_copy(source, target, in_sem.at[i])
        for i, (source, target) in enumerate(
            [
                (kind_hbm, kind), (feat_hbm.at[0], feat), (w_hbm, w), (lw_hbm, lw), (bg_hbm, bg), (bs_hbm, bs),
                (bb_hbm, bb), (fg_hbm, fg), (fs_hbm, fs), (lb_hbm, lb), (ew_hbm, ew), (eb_hbm, eb),
            ]
        )
    ]
    for fetch in fetches:
        fetch.start()
    zsums[...] = jnp.zeros((N_Z, 1, 128), I32)
    got[...] = jnp.zeros((2, 64, 128), BF16)
    lanes[...] = jnp.zeros((8, 128), F32)

    barrier = pltpu.get_barrier_semaphore()

    def greet(target):
        pl.semaphore_signal(barrier, inc=1, device_id=target, device_id_type=MESH)

    for i in range(1, N_X):
        pl.when(i > x)(functools.partial(greet, at_x(i)))
    for i in range(1, N_Z):
        pl.when(i > z)(functools.partial(greet, at_z(i)))
    for i in range(1, N_DP):
        pl.when(i > rank)(functools.partial(greet, {"dp": DP_ORDER[i]}))
    pl.when((x == 0) & (z > 0))(functools.partial(greet, {"seq": seat - 1}))

    block, select = masks()
    for fetch in fetches[:2] + fetches[3:]:
        fetch.wait()
    live = [(kind[0, i] > 0).astype(I32) for i in range(3)]
    n = live[0] + live[1] + live[2]
    kinds = [
        jnp.where(n == 3, kind[0, 2], jnp.where(n == 2, kind[0, 1], kind[0, 0])),
        jnp.where(n == 2, kind[0, 0], kind[0, 1]),
        jnp.where(n == 3, kind[0, 0], kind[0, 2]),
    ]
    joined = [jnp.full((8, C), kinds[t], I32) == 2 for t in range(3)]
    mine[...] = jnp.full((1, 128), n, I32)
    xcounts[pl.ds(x, 1)] = jnp.full((1, 1, 128), n, I32)
    shard[0:64, :] = ew[...]
    bias_row = jnp.broadcast_to(eb[...].reshape(1, 144).astype(F32), (16, 144))
    shard[64:80, :] = jnp.where(iota((16, 144), 0) == 0, bias_row, 0.0).astype(BF16)
    shards[pl.ds(row, 1)] = shard[...].reshape(1, 80, 144)
    lanes[0:1, 0:16] = lb[...]
    lat_bias = lanes[...]
    for step in (16, 32, 64):
        lat_bias = lat_bias + pltpu.roll(lat_bias, step, 1)
    lat_bias = lat_bias[0:1]
    tap_columns(lw, lw3)

    number = jnp.full((16, C), n, I32)
    for i in range(16):
        first, middle, last = [feat[256 * k + 16 * i : 256 * k + 16 * i + 16, :] for k in range(3)]
        part = slice(16 * i, 16 * i + 16)
        slots[0, part, :] = jnp.where(number == 3, last, jnp.where(number == 2, middle, first))
        slots[1, part, :] = jnp.where(number == 2, first, middle)
        slots[2, part, :] = jnp.where(number == 3, first, last)

    def loader(t):
        def load(r):
            return slots[t, 8 * r : 8 * r + 8, :].astype(F32), slots[t, 128 + 8 * r : 136 + 8 * r, :].astype(F32)

        return load

    def inner_loader(t):
        def load(r):
            v = inner[t, 16 * r : 16 * r + 16, :].astype(F32)
            return v[:8], v[8:]

        return load

    def first_norm(t):
        norm_first(loader(t), block, joined[t], bg[...], bs[...], pad.at[t])

    def convolve(t):
        conv(pad.at[t], w, res.at[t])

    def finish(t):
        residual(loader(t), res.at[t], jnp.broadcast_to(bb[...], (8, C)), inner.at[t])
        norm_second(inner_loader(t), block, joined[t], fg[...], fs[...], act.at[t])
        sent[t] = latent_patches(act.at[t], lw3[...], lat_bias, joined[t], select)

    def copy_to(source, target, send_sem, recv_sem, device):
        return pltpu.make_async_remote_copy(
            src_ref=source, dst_ref=target, send_sem=send_sem, recv_sem=recv_sem,
            device_id=device, device_id_type=MESH,
        )

    x_copies = [copy_to(mine, xcounts.at[x], x_send.at[i], x_recv.at[x], at_x(i)) for i in range(N_X)]
    x_arrivals = [copy_to(mine, xcounts.at[i], x_send.at[i], x_recv.at[i], at_x(i)) for i in range(N_X)]
    z_copies = [copy_to(rowsum, zsums.at[z], z_send.at[i], z_recv.at[z], at_z(i)) for i in range(N_Z)]
    z_arrivals = [copy_to(rowsum, zsums.at[i], z_send.at[i], z_recv.at[i], at_z(i)) for i in range(N_Z)]
    d_peers = [{"dp": DP_ORDER[i]} for i in range(N_DP)]
    d_copies = [copy_to(shard, shards.at[row], d_send.at[i], d_recv.at[rank], d_peers[i]) for i in range(N_DP)]
    d_arrivals = [
        copy_to(shard, shards.at[DP_ORDER[i]], d_send.at[i], d_recv.at[i], d_peers[i]) for i in range(N_DP)
    ]
    p_copies = [
        copy_to(sent.at[t], got.at[t], p_send.at[t], p_recv.at[t], {"seq": lax.rem(seat + 1, N_Z * N_X)})
        for t in range(2)
    ]

    def send_patch(t):
        pl.when(seat < N_Z * N_X - 1)(p_copies[t].start)

    first_norm(0)
    earlier = x + z + rank + ((x == N_X - 1) & (z < N_Z - 1)).astype(I32)

    @pl.when(earlier > 0)
    def _():
        pl.semaphore_wait(barrier, earlier)


    def ready(sem, target):
        pl.semaphore_signal(sem, inc=1, device_id=target, device_id_type=MESH)

    for i in range(N_X - 1):
        pl.when(i < x)(functools.partial(ready, x_ready.at[x], at_x(i)))
    for i in range(N_Z - 1):
        pl.when(i < z)(functools.partial(ready, z_ready.at[z], at_z(i)))
    for i in range(N_DP - 1):
        pl.when(i < rank)(functools.partial(ready, d_ready.at[rank], d_peers[i]))
    exchange([(i < x, x_copies[i], None) for i in range(N_X - 1)], True)
    exchange([(i < rank, d_copies[i], None) for i in range(N_DP - 1)], True)

    first_norm(1)
    fetches[2].wait()
    convolve(0)
    first_norm(2)
    exchange([(i > x, x_copies[i], x_ready.at[i]) for i in range(1, N_X)], False)
    exchange([(i > rank, d_copies[i], d_ready.at[i]) for i in range(1, N_DP)], False)

    convolve(1)
    finish(0)
    send_patch(0)

    for i in range(N_X):
        pl.when(i != x)(x_arrivals[i].wait_recv)
    rowsum[...] = jnp.sum(xcounts[...], axis=0)
    exchange([((i > z) & (i < z + 4), z_copies[i], z_ready.at[i]) for i in range(1, N_Z)], False)

    convolve(2)
    finish(1)
    send_patch(1)

    exchange([(i >= z + 4, z_copies[i], z_ready.at[i]) for i in range(4, N_Z)], False)
    for i in range(N_DP):
        pl.when(i != rank)(d_arrivals[i].wait_recv)
    for i in range(N_DP):
        embed_out[:, 144 * i : 144 * i + 144] = shards[i]

    finish(2)
    for i in range(N_Z - 1):
        pl.when(i < z)(z_arrivals[i].wait_recv)
    before = jnp.where(iota((N_X, 1, 128), 0) < x, xcounts[...], 0)
    carry_in = jnp.sum(zsums[...], axis=0) + jnp.sum(before, axis=0) - 2 * seat
    for i in range(N_X):
        pl.when(i != x)(x_arrivals[i].wait_send)
    for i in range(N_DP):
        pl.when(i != rank)(d_arrivals[i].wait_send)
    for i in range(1, N_Z):
        pl.when(i > z)(z_arrivals[i].wait_send)
    for t in range(2):
        pl.when(seat < N_Z * N_X - 1)(p_copies[t].wait_send)
    for t in range(2):
        pl.when(seat > 0)(p_copies[t].wait_recv)

    carry_in = jnp.broadcast_to(carry_in, (64, 128))
    number = jnp.full((64, 128), n, I32)
    own = [sent[t].astype(F32) for t in range(3)]
    came = [got[t].astype(F32) for t in range(2)]
    newest = jnp.where(number == 3, own[2], jnp.where(number == 2, own[1], own[0]))
    second = jnp.where(number == 3, own[1], own[0])
    out0 = jnp.where(carry_in == 0, newest, jnp.where(carry_in == 1, came[0], came[1]))
    out1 = jnp.where(carry_in == 0, second, jnp.where(carry_in == 1, newest, came[0]))
    patches = jnp.concatenate([out0, out1], axis=0)
    patches = jnp.where(iota((128, 128), 1) == 64, 1.0, patches).astype(BF16)
    patch_out[...] = patches[:, :80]


def local(feat, kind, bg, bs, w, bb, fg, fs, lw, lb, ew, eb):
    hbm = pl.BlockSpec(memory_space=pl.ANY)
    vmem = pl.BlockSpec(memory_space=pltpu.VMEM)
    dma, regular, V = pltpu.SemaphoreType.DMA, pltpu.SemaphoreType.REGULAR, pltpu.VMEM
    vec = V((1, C), F32)
    patches, embed = pl.pallas_call(
        kernel,
        out_shape=(jax.ShapeDtypeStruct((128, 80), BF16), jax.ShapeDtypeStruct((80, HID), BF16)),
        in_specs=[hbm] * 12,
        out_specs=(vmem, vmem),
        scratch_shapes=[
            pltpu.SMEM((1, 3), I32), V((768, C), BF16), vec, vec, V((9 * C, C), BF16), vec, vec, vec,
            V((144, C), BF16), V((1, 16), F32), V((64, 144), BF16), V((144,), BF16),
            V((3, 256, C), BF16), V((3, 3, 288, C), BF16), V((3, 256, C), F32), V((3, 256, C), BF16),
            V((3, 256, C), BF16), V((C, 384), BF16), V((8, 128), F32), V((1, 128), I32), V((1, 128), I32),
            V((N_X, 1, 128), I32), V((N_Z, 1, 128), I32), V((80, 144), BF16), V((N_DP, 80, 144), BF16),
            V((3, 64, 128), BF16), V((2, 64, 128), BF16),
            dma((12,)), dma((N_X,)), dma((N_X,)), dma((N_Z,)), dma((N_Z,)), dma((N_DP,)), dma((N_DP,)),
            dma((2,)), dma((2,)), regular((N_X,)), regular((N_Z,)), regular((N_DP,)),
        ],
        compiler_params=pltpu.CompilerParams(
            collective_id=0, has_side_effects=True, vmem_limit_bytes=60 << 20
        ),
    )(
        kind, feat, bg.reshape(1, C), bs.reshape(1, C), w, bb.reshape(1, C), fg.reshape(1, C),
        fs.reshape(1, C), lw.T, lb.reshape(1, 16), ew, eb,
    )
    return jnp.dot(patches, embed, preferred_element_type=F32).astype(BF16)[None]


def solution(mesh):
    shared = P()
    return jax.shard_map(
        local,
        mesh=mesh,
        in_specs=(P("dp", "seq", None), P("dp", "seq")) + (shared,) * 8 + (P(None, "dp"), P("dp")),
        out_specs=P("dp", "seq", None),
        check_vma=False,
    )
```

time: 25.7 us -> 19.3 us (0.75)
  the two profiles are of different devices: /device:TPU:1 before, /device:TPU:224 now
where the time goes in v2:
time: 19.3 us; the launch traced here: 19.2 us
  Pallas kernels  17.3 us (90%)
  matrix products  1.88 us (10%)
    pallas_call x1, Pallas kernels, local(): pl.pallas_call(kernel, out_shape=(jax.ShapeDtypeStruct((128, 80), BF16),...  17.3 us
    dot_general x1, matrix products, local(): jnp.dot(patches, embed, preferred_element_type=F32).astype(BF16)[None]  1.88 us

profile of v2, /device:TPU:224, one launch (start us, length us, event | category | flops | bytes accessed | tf_op | source)
XLA Modules:
  0.0 19.2 jit_solution(3769517995259118437)
XLA Ops:
  0.0 17.3 %shard_map.118 = (bf16[128,80]{1,0:T(8,128)(2,1)}, bf16[80,1152]{1,0:T(8,128)(2,1)}) custom-call(s32[1,3]{1,0:T(1,128)} %kind_hbm.1, bf16[1,768,512]{2,1,0:T(8,128)(2,1)} %feat_hbm.1, f32[1,512]{1,0:T(1,128)} %bitcast.12, f32[1,512]{1,0:T(1,128)} %bitcast.13, bf16[4608,512]{1,0:T(8,128)(2,1)} %w_hbm.1, f32[1,512]{1,0:T(1,128)} %bitcast.14, ...), custom_call_target="tpu_custom_call" | custom-call | tf_op jit(solution)/shard_map/pallas_call | solution.py:390
  17.3 1.9 %fusion = bf16[1,128,1152]{2,1,0:T(8,128)(2,1)} fusion(bf16[128,80]{1,0:T(8,128)(2,1)} %get-tuple-element.7, bf16[80,1152]{1,0:T(8,128)(2,1)} %get-tuple-element.8), kind=kOutput, calls=%fused_computation.1 | convolution fusion | flops 23740416 | bytes 499712 | tf_op jit(solution)/shard_map/dot_general | solution.py:412

commit v3 on v2

--- a/solution.py
+++ b/solution.py
@@ -21,81 +21,101 @@
     return lax.broadcasted_iota(I32, shape, dim)
 
 
-def lane_tiles(v):
-    return [v[:, 128 * i : 128 * i + 128] for i in range(v.shape[1] // 128)]
+def drain(*streams):
+    live = [[stream, steps, 0] for stream, steps in streams]
+    while live:
+        entry = min(live, key=lambda e: (e[2] + 1) / e[1])
+        entry[2] += 1
+        try:
+            next(entry[0])
+        except StopIteration:
+            live.remove(entry)
 
 
 def group_sums(parts, block):
-    rows = jnp.concatenate([t for p in parts for t in lane_tiles(p)], axis=0)
+    rows = jnp.concatenate([p[:, 256 * i : 256 * i + 256] for p in parts for i in range(2)], axis=0)
     hi = rows.astype(BF16)
     rest = rows - hi.astype(F32)
     mid = rest.astype(BF16)
     low = (rest - mid.astype(F32)).astype(BF16)
     sums = jnp.dot(jnp.concatenate([hi, mid, low], axis=0), block, preferred_element_type=F32)
-    count = rows.shape[0]
-    total = sums[:count] + sums[count : 2 * count] + sums[2 * count :]
+    total = sums[:32] + sums[32:64] + sums[64:]
     out = []
     for i in range(len(parts)):
-        tiles = []
-        for j in range(4):
-            tile = total[32 * i + 8 * j : 32 * i + 8 * j + 8]
-            tiles.append(jnp.broadcast_to(jnp.sum(tile, axis=0, keepdims=True), (8, 128)))
+        tiles = [total[16 * i + 8 * j : 16 * i + 8 * j + 8] for j in range(2)]
+        tiles = [jnp.broadcast_to(jnp.sum(t, axis=0, keepdims=True), (8, 256)) for t in tiles]
         out.append(jnp.concatenate(tiles, axis=1))
     return out
 
 
-def norm_scales(load, block, joined, gain, shift):
-    zero = jnp.zeros((8, C), F32)
-    low, high = zero, zero
-    for r in range(16):
-        x0, x1 = load(r)
-        low, high = low + x0, high + x1
-    m0, m1 = group_sums([low, high], block)
+def norm_factors(sums, load, block, joined, gain, shift):
+    m0, m1 = group_sums(sums, block)
     m0, m1 = m0 * (1.0 / 2048), m1 * (1.0 / 2048)
     both = (m0 + m1) * 0.5
     c0, c1 = jnp.where(joined, both, m0), jnp.where(joined, both, m1)
-    low, high = zero, zero
+    low, high = jnp.zeros((8, C), F32), jnp.zeros((8, C), F32)
     for r in range(16):
         x0, x1 = load(r)
         x0, x1 = x0 - c0, x1 - c1
         low, high = low + x0 * x0, high + x1 * x1
+        yield
     v0, v1 = group_sums([low, high], block)
     v0, v1 = v0 * (1.0 / 2048), v1 * (1.0 / 2048)
     both = (v0 + v1) * 0.5
     v0, v1 = jnp.where(joined, both, v0), jnp.where(joined, both, v1)
     s0 = lax.rsqrt(v0 + EPS) * gain * 0.5
     s1 = lax.rsqrt(v1 + EPS) * gain * 0.5
-    return c0, c1, s0, s1, jnp.broadcast_to(shift * 0.5, (8, C))
+    return s0, s1, shift * 0.5 - c0 * s0, shift * 0.5 - c1 * s1
 
 
 def silu_half(half):
     return half + half * jnp.tanh(half)
 
 
-def side_shifts(y):
-    col = iota((8, C), 0)
-    left = jnp.where(col >= 1, pltpu.roll(y, 1, 0), 0.0)
-    right = jnp.where(col <= 6, pltpu.roll(y, 7, 0), 0.0)
-    return left, y, right
-
-
 def pair(top, bottom):
     return jnp.concatenate([top, bottom], axis=0).astype(BF16)
 
 
-def norm_first(load, block, joined, gain, shift, pad):
-    c0, c1, s0, s1, t = norm_scales(load, block, joined, gain, shift)
+def loader(ref):
+    def load(r):
+        return ref[16 * r : 16 * r + 8, :], ref[16 * r + 8 : 16 * r + 16, :]
+
+    return load
+
+
+def order_slot(pick, slot):
+    low, high = jnp.zeros((8, C), F32), jnp.zeros((8, C), F32)
+    for i in range(8):
+        top, bottom = pick(16 * i).astype(F32), pick(128 + 16 * i).astype(F32)
+        for j in range(2):
+            x0, x1 = top[8 * j : 8 * j + 8], bottom[8 * j : 8 * j + 8]
+            r = 2 * i + j
+            slot[16 * r : 16 * r + 8, :], slot[16 * r + 8 : 16 * r + 16, :] = x0, x1
+            low, high = low + x0, high + x1
+        yield
+    return low, high
+
+
+def norm_first(pick, slot, block, joined, gain, shift, pad):
+    sums = yield from order_slot(pick, slot)
+    load = loader(slot)
+    s0, s1, t0, t1 = yield from norm_factors(sums, load, block, joined, gain, shift)
     zero = jnp.zeros((8, C), F32)
+    col = iota((8, C), 0)
     for r in range(16):
         x0, x1 = load(r)
-        y0, y1 = silu_half((x0 - c0) * s0 + t), silu_half((x1 - c1) * s1 + t)
-        sides0, sides1 = side_shifts(y0), side_shifts(y1)
+        sides = []
+        for y in (silu_half(x0 * s0 + t0), silu_half(x1 * s1 + t1)):
+            left = jnp.where(col >= 1, pltpu.roll(y, 1, 0), 0.0)
+            right = jnp.where(col <= 6, pltpu.roll(y, 7, 0), 0.0)
+            sides.append((left, y, right))
         for b in range(3):
-            pad[b, 16 * (r + 1) : 16 * (r + 2), :] = pair(sides0[b], sides1[b])
+            pad[b, 16 * (r + 1) : 16 * (r + 2), :] = pair(sides[0][b], sides[1][b])
             if r == 0:
-                pad[b, 16 * 17 : 16 * 18, :] = pair(jnp.where(joined, sides1[b], 0.0), zero)
+                pad[b, 16 * 17 : 16 * 18, :] = pair(jnp.where(joined, sides[1][b], 0.0), zero)
             if r == 15:
-                pad[b, 0:16, :] = pair(zero, jnp.where(joined, sides0[b], 0.0))
+                pad[b, 0:16, :] = pair(zero, jnp.where(joined, sides[0][b], 0.0))
+        yield
 
 
 def conv(pad, w, res):
@@ -105,24 +125,26 @@
     res[...] = jnp.dot(lhs, w[...], preferred_element_type=F32)
 
 
-def residual(load, res, bias, inner):
+def finish(slot, res, bias, block, joined, gain, shift, act, lw3, lat_bias, select, out):
+    own, added = loader(slot), loader(res)
+    low, high = jnp.zeros((8, C), F32), jnp.zeros((8, C), F32)
     for r in range(16):
-        x0, x1 = load(r)
-        top, bottom = res[16 * r : 16 * r + 8, :], res[16 * r + 8 : 16 * r + 16, :]
-        inner[16 * r : 16 * r + 16, :] = pair(top + x0 + bias, bottom + x1 + bias)
-
-
-def norm_second(load, block, joined, gain, shift, act):
-    c0, c1, s0, s1, t = norm_scales(load, block, joined, gain, shift)
+        (x0, x1), (d0, d1) = own(r), added(r)
+        x0, x1 = x0 + d0 + bias, x1 + d1 + bias
+        res[16 * r : 16 * r + 8, :], res[16 * r + 8 : 16 * r + 16, :] = x0, x1
+        low, high = low + x0, high + x1
+        yield
+    s0, s1, t0, t1 = yield from norm_factors([low, high], added, block, joined, gain, shift)
     for r in range(16):
-        x0, x1 = load(r)
-        act[16 * r : 16 * r + 16, :] = pair(
-            silu_half((x0 - c0) * s0 + t), silu_half((x1 - c1) * s1 + t)
-        )
-
-
-def latent_patches(act, lw3, lat_bias, joined, select):
-    terms = jnp.dot(act[...], lw3, preferred_element_type=F32)
+        x0, x1 = added(r)
+        act[16 * r : 16 * r + 16, :] = pair(silu_half(x0 * s0 + t0), silu_half(x1 * s1 + t1))
+        yield
+    yield from latent_patches(act, lw3, lat_bias, joined, select, out)
+
+
+def latent_patches(act, lw3, lat_bias, joined, select, out):
+    terms = jnp.dot(act[...], lw3[...], preferred_element_type=F32)
+    yield
     joined = joined[:, :128]
     zero = jnp.zeros((8, 128), F32)
 
@@ -132,27 +154,24 @@
     col = iota((8, 128), 0)
     lane = iota((8, 128), 1)
     rows = []
-    for p in range(8):
+    for r in range(16):
         for h in range(2):
-            total = None
-            for i in range(2):
-                r = 2 * p + i
-                above = part(-1, r - 1, h) if r > 0 else (jnp.where(joined, part(-1, 15, 0), 0.0) if h == 1 else zero)
-                below = part(1, r + 1, h) if r < 15 else (jnp.where(joined, part(1, 0, 1), 0.0) if h == 0 else zero)
-                z = above + part(0, r, h) + below
-                left = jnp.where(col >= 1, pltpu.roll(z, 1, 0), 0.0)
-                right = jnp.where(col <= 6, pltpu.roll(z, 7, 0), 0.0)
-                if i == 0:
-                    lat = left + pltpu.roll(z, 96, 1) + pltpu.roll(right, 64, 1)
-                else:
-                    lat = pltpu.roll(left, 32, 1) + z + pltpu.roll(right, 96, 1)
-                lat = (lat + lat_bias - LATENT_SHIFT) * LATENT_SCALE
-                own = (lane // 16) == (2 * i + col % 2)
-                lat = jnp.where(own, lat, 0.0)
-                total = lat if total is None else total + lat
-            rows.append(total)
+            i = r % 2
+            above = part(-1, r - 1, h) if r > 0 else (jnp.where(joined, part(-1, 15, 0), 0.0) if h == 1 else zero)
+            below = part(1, r + 1, h) if r < 15 else (jnp.where(joined, part(1, 0, 1), 0.0) if h == 0 else zero)
+            v = above + part(0, r, h) + below
+            left = jnp.where(col >= 1, pltpu.roll(v, 1, 0), 0.0)
+            right = jnp.where(col <= 6, pltpu.roll(v, 7, 0), 0.0)
+            if i == 0:
+                lat = left + pltpu.roll(v, 96, 1) + pltpu.roll(right, 64, 1)
+            else:
+                lat = pltpu.roll(left, 32, 1) + v + pltpu.roll(right, 96, 1)
+            lat = (lat + lat_bias - LATENT_SHIFT) * LATENT_SCALE
+            rows.append(jnp.where((lane // 16) == (2 * i + col % 2), lat, 0.0))
+        if r % 2:
+            yield
     cells = jnp.concatenate(rows, axis=0).astype(BF16)
-    return jnp.dot(select, cells, preferred_element_type=F32).astype(BF16)
+    out[...] = jnp.dot(select, cells, preferred_element_type=F32).astype(BF16)
 
 
 def tap_columns(lwt, lw3):
@@ -164,13 +183,13 @@
 
 
 def masks():
-    block = jnp.where(iota((128, 128), 0) // 16 == iota((128, 128), 1) // 16, 1.0, 0.0).astype(BF16)
-    t, m = iota((64, 128), 0), iota((64, 128), 1)
-    same = (m // 16 == (t // 4) % 8) & ((m // 8) % 2 == t // 32) & ((m % 8) // 2 == t % 4)
+    block = jnp.where(iota((256, 256), 0) // 16 == iota((256, 256), 1) // 16, 1.0, 0.0).astype(BF16)
+    t, m = iota((64, 256), 0), iota((64, 256), 1)
+    same = (m // 32 == (t // 4) % 8) & ((m // 8) % 2 == t // 32) & ((m % 8) // 2 == t % 4)
     return block, jnp.where(same, 1.0, 0.0).astype(BF16)
 
 
-DP_ORDER = (6, 4, 2, 7, 5, 3, 1, 0)
+DP_ORDER = (0, 1, 2, 6, 3, 7, 4, 5)
 
 
 def exchange(pairs, start_now):
@@ -187,12 +206,12 @@
     kind_hbm, feat_hbm, bg_hbm, bs_hbm, w_hbm, bb_hbm, fg_hbm, fs_hbm, lw_hbm, lb_hbm, ew_hbm, eb_hbm,
     patch_out, embed_out,
     kind, feat, bg, bs, w, bb, fg, fs, lw, lb, ew, eb,
-    slots, pad, res, inner, act, lw3, lanes, mine, rowsum, xcounts, zsums, shard, shards, sent, got,
+    slots, pad, res, act, lw3, lanes, mine, rowsum, xcounts, zsums, shard, shards, sent, got,
     in_sem, x_send, x_recv, z_send, z_recv, d_send, d_recv, p_send, p_recv, x_ready, z_ready, d_ready,
 ):
     seat, row = lax.axis_index("seq"), lax.axis_index("dp")
     z, x = seat // N_X, lax.rem(seat, N_X)
-    rank = jnp.where(row == 0, 7, jnp.where(lax.rem(row, 2) == 0, 3 - row // 2, 6 - row // 2))
+    rank = sum(jnp.where(row == DP_ORDER[i], i, 0) for i in range(N_DP))
 
     def at_x(i):
         return {"seq": z * N_X + i}
@@ -250,39 +269,36 @@
     for step in (16, 32, 64):
         lat_bias = lat_bias + pltpu.roll(lat_bias, step, 1)
     lat_bias = lat_bias[0:1]
-    tap_columns(lw, lw3)
 
     number = jnp.full((16, C), n, I32)
-    for i in range(16):
-        first, middle, last = [feat[256 * k + 16 * i : 256 * k + 16 * i + 16, :] for k in range(3)]
-        part = slice(16 * i, 16 * i + 16)
-        slots[0, part, :] = jnp.where(number == 3, last, jnp.where(number == 2, middle, first))
-        slots[1, part, :] = jnp.where(number == 2, first, middle)
-        slots[2, part, :] = jnp.where(number == 3, first, last)
-
-    def loader(t):
-        def load(r):
-            return slots[t, 8 * r : 8 * r + 8, :].astype(F32), slots[t, 128 + 8 * r : 136 + 8 * r, :].astype(F32)
-
-        return load
-
-    def inner_loader(t):
-        def load(r):
-            v = inner[t, 16 * r : 16 * r + 16, :].astype(F32)
-            return v[:8], v[8:]
-
-        return load
+
+    def cells(k, i):
+        return feat[256 * k + i : 256 * k + i + 16, :]
+
+    def pick(t):
+        def rows(i):
+            if t == 0:
+                return jnp.where(number == 3, cells(2, i), jnp.where(number == 2, cells(1, i), cells(0, i)))
+            if t == 1:
+                return jnp.where(number == 2, cells(0, i), cells(1, i))
+            return jnp.where(number == 3, cells(0, i), cells(2, i))
+
+        return rows
+
+    def spread(vector):
+        return jnp.broadcast_to(vector[...], (8, C))
 
     def first_norm(t):
-        norm_first(loader(t), block, joined[t], bg[...], bs[...], pad.at[t])
+        return norm_first(pick(t), slots.at[t], block, joined[t], spread(bg), spread(bs), pad.at[t])
 
     def convolve(t):
         conv(pad.at[t], w, res.at[t])
 
-    def finish(t):
-        residual(loader(t), res.at[t], jnp.broadcast_to(bb[...], (8, C)), inner.at[t])
-        norm_second(inner_loader(t), block, joined[t], fg[...], fs[...], act.at[t])
-        sent[t] = latent_patches(act.at[t], lw3[...], lat_bias, joined[t], select)
+    def last(t):
+        return finish(
+            slots.at[t], res.at[t], spread(bb), block, joined[t], spread(fg), spread(fs), act.at[t],
+            lw3, lat_bias, select, sent.at[t],
+        )
 
     def copy_to(source, target, send_sem, recv_sem, device):
         return pltpu.make_async_remote_copy(
@@ -307,7 +323,6 @@
     def send_patch(t):
         pl.when(seat < N_Z * N_X - 1)(p_copies[t].start)
 
-    first_norm(0)
     earlier = x + z + rank + ((x == N_X - 1) & (z < N_Z - 1)).astype(I32)
 
     @pl.when(earlier > 0)
@@ -327,33 +342,30 @@
     exchange([(i < x, x_copies[i], None) for i in range(N_X - 1)], True)
     exchange([(i < rank, d_copies[i], None) for i in range(N_DP - 1)], True)
 
-    first_norm(1)
+    tap_columns(lw, lw3)
+    drain((first_norm(0), 42), (first_norm(1), 42))
     fetches[2].wait()
     convolve(0)
-    first_norm(2)
+    drain((last(0), 60), (first_norm(2), 42))
     exchange([(i > x, x_copies[i], x_ready.at[i]) for i in range(1, N_X)], False)
+    send_patch(0)
+
+    convolve(1)
     exchange([(i > rank, d_copies[i], d_ready.at[i]) for i in range(1, N_DP)], False)
-
-    convolve(1)
-    finish(0)
-    send_patch(0)
-
     for i in range(N_X):
         pl.when(i != x)(x_arrivals[i].wait_recv)
     rowsum[...] = jnp.sum(xcounts[...], axis=0)
     exchange([((i > z) & (i < z + 4), z_copies[i], z_ready.at[i]) for i in range(1, N_Z)], False)
+    drain((last(1), 60))
+    send_patch(1)
 
     convolve(2)
-    finish(1)
-    send_patch(1)
-
     exchange([(i >= z + 4, z_copies[i], z_ready.at[i]) for i in range(4, N_Z)], False)
     for i in range(N_DP):
         pl.when(i != rank)(d_arrivals[i].wait_recv)
     for i in range(N_DP):
         embed_out[:, 144 * i : 144 * i + 144] = shards[i]
-
-    finish(2)
+    drain((last(2), 60))
     for i in range(N_Z - 1):
         pl.when(i < z)(z_arrivals[i].wait_recv)
     before = jnp.where(iota((N_X, 1, 128), 0) < x, xcounts[...], 0)
@@ -395,8 +407,8 @@
         scratch_shapes=[
             pltpu.SMEM((1, 3), I32), V((768, C), BF16), vec, vec, V((9 * C, C), BF16), vec, vec, vec,
             V((144, C), BF16), V((1, 16), F32), V((64, 144), BF16), V((144,), BF16),
-            V((3, 256, C), BF16), V((3, 3, 288, C), BF16), V((3, 256, C), F32), V((3, 256, C), BF16),
-            V((3, 256, C), BF16), V((C, 384), BF16), V((8, 128), F32), V((1, 128), I32), V((1, 128), I32),
+            V((3, 256, C), F32), V((3, 3, 288, C), BF16), V((3, 256, C), F32), V((3, 256, C), BF16),
+            V((C, 384), BF16), V((8, 128), F32), V((1, 128), I32), V((1, 128), I32),
             V((N_X, 1, 128), I32), V((N_Z, 1, 128), I32), V((80, 144), BF16), V((N_DP, 80, 144), BF16),
             V((3, 64, 128), BF16), V((2, 64, 128), BF16),
             dma((12,)), dma((N_X,)), dma((N_X,)), dma((N_Z,)), dma((N_Z,)), dma((N_DP,)), dma((N_DP,)),

time: 19.3 us -> 18.4 us (0.953)
  Pallas kernels: 17.3 us -> 16.4 us
    pallas_call x1, Pallas kernels: 17.3 us -> 16.4 us  [local(): pl.pallas_call(kernel, out_shape=(jax.ShapeDtypeStruct((128, 80), BF16),...]
where the time goes in v3:
time: 18.4 us; the launch traced here: 18.3 us
  Pallas kernels  16.4 us (89%)
  matrix products  1.87 us (10%)
    pallas_call x1, Pallas kernels, local(): pl.pallas_call(kernel, out_shape=(jax.ShapeDtypeStruct((128, 80), BF16),...  16.4 us
    dot_general x1, matrix products, local(): jnp.dot(patches, embed, preferred_element_type=F32).astype(BF16)[None]  1.87 us

profile of v3, /device:TPU:224, one launch (start us, length us, event | category | flops | bytes accessed | tf_op | source)
XLA Modules:
  0.0 18.3 jit_solution(4940476488166664948)
XLA Ops:
  0.0 16.4 %shard_map.118 = (bf16[128,80]{1,0:T(8,128)(2,1)}, bf16[80,1152]{1,0:T(8,128)(2,1)}) custom-call(s32[1,3]{1,0:T(1,128)} %kind_hbm.1, bf16[1,768,512]{2,1,0:T(8,128)(2,1)} %feat_hbm.1, f32[1,512]{1,0:T(1,128)} %bitcast.12, f32[1,512]{1,0:T(1,128)} %bitcast.13, bf16[4608,512]{1,0:T(8,128)(2,1)} %w_hbm.1, f32[1,512]{1,0:T(1,128)} %bitcast.14, ...), custom_call_target="tpu_custom_call" | custom-call | tf_op jit(solution)/shard_map/pallas_call | solution.py:402
  16.4 1.9 %fusion = bf16[1,128,1152]{2,1,0:T(8,128)(2,1)} fusion(bf16[128,80]{1,0:T(8,128)(2,1)} %get-tuple-element.7, bf16[80,1152]{1,0:T(8,128)(2,1)} %get-tuple-element.8), kind=kOutput, calls=%fused_computation.1 | convolution fusion | flops 23740416 | bytes 499712 | tf_op jit(solution)/shard_map/dot_general | solution.py:424

commit v4 on v3

--- a/solution.py
+++ b/solution.py
@@ -346,7 +346,7 @@
     drain((first_norm(0), 42), (first_norm(1), 42))
     fetches[2].wait()
     convolve(0)
-    drain((last(0), 60), (first_norm(2), 42))
+    drain((last(0), 60))
     exchange([(i > x, x_copies[i], x_ready.at[i]) for i in range(1, N_X)], False)
     send_patch(0)
 
@@ -358,14 +358,15 @@
     exchange([((i > z) & (i < z + 4), z_copies[i], z_ready.at[i]) for i in range(1, N_Z)], False)
     drain((last(1), 60))
     send_patch(1)
-
+    exchange([(i >= z + 4, z_copies[i], z_ready.at[i]) for i in range(4, N_Z)], False)
+
+    drain((first_norm(2), 42))
     convolve(2)
-    exchange([(i >= z + 4, z_copies[i], z_ready.at[i]) for i in range(4, N_Z)], False)
+    drain((last(2), 60))
     for i in range(N_DP):
         pl.when(i != rank)(d_arrivals[i].wait_recv)
     for i in range(N_DP):
         embed_out[:, 144 * i : 144 * i + 144] = shards[i]
-    drain((last(2), 60))
     for i in range(N_Z - 1):
         pl.when(i < z)(z_arrivals[i].wait_recv)
     before = jnp.where(iota((N_X, 1, 128), 0) < x, xcounts[...], 0)

time: 18.4 us -> 18.3 us (level)
  no operation moved by 1% of the time
where the time goes in v4:
time: 18.3 us; the launch traced here: 18.2 us
  Pallas kernels  16.3 us (89%)
  matrix products  1.87 us (10%)
    pallas_call x1, Pallas kernels, local(): pl.pallas_call(kernel, out_shape=(jax.ShapeDtypeStruct((128, 80), BF16),...  16.3 us
    dot_general x1, matrix products, local(): jnp.dot(patches, embed, preferred_element_type=F32).astype(BF16)[None]  1.87 us

profile of v4, /device:TPU:224, one launch (start us, length us, event | category | flops | bytes accessed | tf_op | source)
XLA Modules:
  0.0 18.2 jit_solution(6596972971001486410)
XLA Ops:
  0.0 16.3 %shard_map.118 = (bf16[128,80]{1,0:T(8,128)(2,1)}, bf16[80,1152]{1,0:T(8,128)(2,1)}) custom-call(s32[1,3]{1,0:T(1,128)} %kind_hbm.1, bf16[1,768,512]{2,1,0:T(8,128)(2,1)} %feat_hbm.1, f32[1,512]{1,0:T(1,128)} %bitcast.12, f32[1,512]{1,0:T(1,128)} %bitcast.13, bf16[4608,512]{1,0:T(8,128)(2,1)} %w_hbm.1, f32[1,512]{1,0:T(1,128)} %bitcast.14, ...), custom_call_target="tpu_custom_call" | custom-call | tf_op jit(solution)/shard_map/pallas_call | solution.py:403
  16.3 1.9 %fusion = bf16[1,128,1152]{2,1,0:T(8,128)(2,1)} fusion(bf16[128,80]{1,0:T(8,128)(2,1)} %get-tuple-element.7, bf16[80,1152]{1,0:T(8,128)(2,1)} %get-tuple-element.8), kind=kOutput, calls=%fused_computation.1 | convolution fusion | flops 23740416 | bytes 499712 | tf_op jit(solution)/shard_map/dot_general | solution.py:425

commit v5 on v4

--- a/solution.py
+++ b/solution.py
@@ -352,12 +352,17 @@
 
     convolve(1)
     exchange([(i > rank, d_copies[i], d_ready.at[i]) for i in range(1, N_DP)], False)
-    for i in range(N_X):
-        pl.when(i != x)(x_arrivals[i].wait_recv)
-    rowsum[...] = jnp.sum(xcounts[...], axis=0)
-    exchange([((i > z) & (i < z + 4), z_copies[i], z_ready.at[i]) for i in range(1, N_Z)], False)
+
+    def row_sums():
+        for i in range(N_X):
+            pl.when(i != x)(x_arrivals[i].wait_recv)
+        rowsum[...] = jnp.sum(xcounts[...], axis=0)
+        exchange([((i > z) & (i < z + 4), z_copies[i], z_ready.at[i]) for i in range(1, N_Z)], False)
+
+    pl.when(x < 2)(row_sums)
     drain((last(1), 60))
     send_patch(1)
+    pl.when(x >= 2)(row_sums)
     exchange([(i >= z + 4, z_copies[i], z_ready.at[i]) for i in range(4, N_Z)], False)
 
     drain((first_norm(2), 42))
@@ -393,6 +398,10 @@
     patches = jnp.concatenate([out0, out1], axis=0)
     patches = jnp.where(iota((128, 128), 1) == 64, 1.0, patches).astype(BF16)
     patch_out[...] = patches[:, :80]
+
+
+def embed_patches(patches, embed, out):
+    out[0] = jnp.dot(patches[...], embed[...], preferred_element_type=F32).astype(BF16)
 
 
 def local(feat, kind, bg, bs, w, bb, fg, fs, lw, lb, ew, eb):
@@ -422,7 +431,12 @@
         kind, feat, bg.reshape(1, C), bs.reshape(1, C), w, bb.reshape(1, C), fg.reshape(1, C),
         fs.reshape(1, C), lw.T, lb.reshape(1, 16), ew, eb,
     )
-    return jnp.dot(patches, embed, preferred_element_type=F32).astype(BF16)[None]
+    return pl.pallas_call(
+        embed_patches,
+        out_shape=jax.ShapeDtypeStruct((1, 128, HID), BF16),
+        in_specs=[vmem, vmem],
+        out_specs=vmem,
+    )(patches, embed)
 
 
 def solution(mesh):

time: 18.3 us -> 17.1 us (0.934)
  the two profiles are of different devices: /device:TPU:224 before, /device:TPU:2 now
where the time goes in v5:
time: 17.1 us; the launch traced here: 17 us
  Pallas kernels  17 us (99%)
    pallas_call x1, Pallas kernels, local(): pl.pallas_call(kernel, out_shape=(jax.ShapeDtypeStruct((128, 80), BF16),...  15.2 us
    pallas_call x1, Pallas kernels, local(): pl.pallas_call(embed_patches, out_shape=jax.ShapeDtypeStruct((1, 128, HID...  1.88 us

profile of v5, /device:TPU:2, one launch (start us, length us, event | category | flops | bytes accessed | tf_op | source)
XLA Modules:
  0.0 17.0 jit_solution(13993581364672180539)
XLA Ops:
  0.0 15.2 %shard_map.118 = (bf16[128,80]{1,0:T(8,128)(2,1)}, bf16[80,1152]{1,0:T(8,128)(2,1)}) custom-call(s32[1,3]{1,0:T(1,128)} %kind_hbm.1, bf16[1,768,512]{2,1,0:T(8,128)(2,1)} %feat_hbm.1, f32[1,512]{1,0:T(1,128)} %bitcast.8, f32[1,512]{1,0:T(1,128)} %bitcast.9, bf16[4608,512]{1,0:T(8,128)(2,1)} %w_hbm.1, f32[1,512]{1,0:T(1,128)} %bitcast.10, f32[1,512]{1,0:T(1,128)} %bitcast.11, ...), custom_call_target="tpu_custom_call" | custom-call | tf_op jit(solution)/shard_map/pallas_call | solution.py:412
  15.2 1.9 %shard_map.119 = bf16[1,128,1152]{2,1,0:T(8,128)(2,1)} custom-call(bf16[128,80]{1,0:T(8,128)(2,1)} %get-tuple-element.7.patches, bf16[80,1152]{1,0:T(8,128)(2,1)} %get-tuple-element.8.embed), custom_call_target="tpu_custom_call" | custom-call | tf_op jit(solution)/shard_map/pallas_call | solution.py:434

commit v6 on v5

--- a/solution.py
+++ b/solution.py
@@ -323,6 +323,8 @@
     def send_patch(t):
         pl.when(seat < N_Z * N_X - 1)(p_copies[t].start)
 
+    tap_columns(lw, lw3)
+    drain((first_norm(0), 42), (first_norm(1), 42))
     earlier = x + z + rank + ((x == N_X - 1) & (z < N_Z - 1)).astype(I32)
 
     @pl.when(earlier > 0)
@@ -342,31 +344,21 @@
     exchange([(i < x, x_copies[i], None) for i in range(N_X - 1)], True)
     exchange([(i < rank, d_copies[i], None) for i in range(N_DP - 1)], True)
 
-    tap_columns(lw, lw3)
-    drain((first_norm(0), 42), (first_norm(1), 42))
     fetches[2].wait()
     convolve(0)
-    drain((last(0), 60))
+    convolve(1)
     exchange([(i > x, x_copies[i], x_ready.at[i]) for i in range(1, N_X)], False)
-    send_patch(0)
-
-    convolve(1)
     exchange([(i > rank, d_copies[i], d_ready.at[i]) for i in range(1, N_DP)], False)
-
-    def row_sums():
-        for i in range(N_X):
-            pl.when(i != x)(x_arrivals[i].wait_recv)
-        rowsum[...] = jnp.sum(xcounts[...], axis=0)
-        exchange([((i > z) & (i < z + 4), z_copies[i], z_ready.at[i]) for i in range(1, N_Z)], False)
-
-    pl.when(x < 2)(row_sums)
-    drain((last(1), 60))
-    send_patch(1)
-    pl.when(x >= 2)(row_sums)
-    exchange([(i >= z + 4, z_copies[i], z_ready.at[i]) for i in range(4, N_Z)], False)
+    drain((last(0), 60), (last(1), 60))
+    for t in range(2):
+        send_patch(t)
 
     drain((first_norm(2), 42))
     convolve(2)
+    for i in range(N_X):
+        pl.when(i != x)(x_arrivals[i].wait_recv)
+    rowsum[...] = jnp.sum(xcounts[...], axis=0)
+    exchange([(i > z, z_copies[i], z_ready.at[i]) for i in range(1, N_Z)], False)
     drain((last(2), 60))
     for i in range(N_DP):
         pl.when(i != rank)(d_arrivals[i].wait_recv)

time: 17.1 us -> 16.8 us (0.982)
  the two profiles are of different devices: /device:TPU:2 before, /device:TPU:224 now
where the time goes in v6:
time: 16.8 us; the launch traced here: 16.7 us
  Pallas kernels  16.7 us (99%)
    pallas_call x1, Pallas kernels, local(): pl.pallas_call(kernel, out_shape=(jax.ShapeDtypeStruct((128, 80), BF16),...  14.8 us
    pallas_call x1, Pallas kernels, local(): pl.pallas_call(embed_patches, out_shape=jax.ShapeDtypeStruct((1, 128, HID...  1.88 us

profile of v6, /device:TPU:224, one launch (start us, length us, event | category | flops | bytes accessed | tf_op | source)
XLA Modules:
  0.0 16.7 jit_solution(15738008474411971677)
XLA Ops:
  0.0 14.8 %shard_map.118 = (bf16[128,80]{1,0:T(8,128)(2,1)}, bf16[80,1152]{1,0:T(8,128)(2,1)}) custom-call(s32[1,3]{1,0:T(1,128)} %kind_hbm.1, bf16[1,768,512]{2,1,0:T(8,128)(2,1)} %feat_hbm.1, f32[1,512]{1,0:T(1,128)} %bitcast.8, f32[1,512]{1,0:T(1,128)} %bitcast.9, bf16[4608,512]{1,0:T(8,128)(2,1)} %w_hbm.1, f32[1,512]{1,0:T(1,128)} %bitcast.10, f32[1,512]{1,0:T(1,128)} %bitcast.11, ...), custom_call_target="tpu_custom_call" | custom-call | tf_op jit(solution)/shard_map/pallas_call | solution.py:404
  14.8 1.9 %shard_map.119 = bf16[1,128,1152]{2,1,0:T(8,128)(2,1)} custom-call(bf16[128,80]{1,0:T(8,128)(2,1)} %get-tuple-element.7.patches, bf16[80,1152]{1,0:T(8,128)(2,1)} %get-tuple-element.8.embed), custom_call_target="tpu_custom_call" | custom-call | tf_op jit(solution)/shard_map/pallas_call | solution.py:426

commit v7 on v6

--- a/solution.py
+++ b/solution.py
@@ -223,8 +223,8 @@
         pltpu.make_async_copy(source, target, in_sem.at[i])
         for i, (source, target) in enumerate(
             [
-                (kind_hbm, kind), (feat_hbm.at[0], feat), (w_hbm, w), (lw_hbm, lw), (bg_hbm, bg), (bs_hbm, bs),
-                (bb_hbm, bb), (fg_hbm, fg), (fs_hbm, fs), (lb_hbm, lb), (ew_hbm, ew), (eb_hbm, eb),
+                (kind_hbm, kind), (lw_hbm, lw), (bg_hbm, bg), (bs_hbm, bs), (bb_hbm, bb), (fg_hbm, fg),
+                (fs_hbm, fs), (lb_hbm, lb), (ew_hbm, ew), (eb_hbm, eb), (feat_hbm.at[0], feat), (w_hbm, w),
             ]
         )
     ]
@@ -239,16 +239,16 @@
     def greet(target):
         pl.semaphore_signal(barrier, inc=1, device_id=target, device_id_type=MESH)
 
+    for i in range(1, N_DP):
+        pl.when(i > rank)(functools.partial(greet, {"dp": DP_ORDER[i]}))
     for i in range(1, N_X):
         pl.when(i > x)(functools.partial(greet, at_x(i)))
+    pl.when((x == 0) & (z > 0))(functools.partial(greet, {"seq": seat - 1}))
     for i in range(1, N_Z):
         pl.when(i > z)(functools.partial(greet, at_z(i)))
-    for i in range(1, N_DP):
-        pl.when(i > rank)(functools.partial(greet, {"dp": DP_ORDER[i]}))
-    pl.when((x == 0) & (z > 0))(functools.partial(greet, {"seq": seat - 1}))
 
     block, select = masks()
-    for fetch in fetches[:2] + fetches[3:]:
+    for fetch in fetches[:10]:
         fetch.wait()
     live = [(kind[0, i] > 0).astype(I32) for i in range(3)]
     n = live[0] + live[1] + live[2]
@@ -324,6 +324,7 @@
         pl.when(seat < N_Z * N_X - 1)(p_copies[t].start)
 
     tap_columns(lw, lw3)
+    fetches[10].wait()
     drain((first_norm(0), 42), (first_norm(1), 42))
     earlier = x + z + rank + ((x == N_X - 1) & (z < N_Z - 1)).astype(I32)
 
@@ -344,7 +345,7 @@
     exchange([(i < x, x_copies[i], None) for i in range(N_X - 1)], True)
     exchange([(i < rank, d_copies[i], None) for i in range(N_DP - 1)], True)
 
-    fetches[2].wait()
+    fetches[11].wait()
     convolve(0)
     convolve(1)
     exchange([(i > x, x_copies[i], x_ready.at[i]) for i in range(1, N_X)], False)
@@ -354,11 +355,11 @@
         send_patch(t)
 
     drain((first_norm(2), 42))
-    convolve(2)
     for i in range(N_X):
         pl.when(i != x)(x_arrivals[i].wait_recv)
     rowsum[...] = jnp.sum(xcounts[...], axis=0)
     exchange([(i > z, z_copies[i], z_ready.at[i]) for i in range(1, N_Z)], False)
+    convolve(2)
     drain((last(2), 60))
     for i in range(N_DP):
         pl.when(i != rank)(d_arrivals[i].wait_recv)

time: 16.8 us -> 15.9 us (0.946)
  the two profiles are of different devices: /device:TPU:224 before, /device:TPU:1 now
where the time goes in v7:
time: 15.9 us; the launch traced here: 15.8 us
  Pallas kernels  15.8 us (99%)
    pallas_call x1, Pallas kernels, local(): pl.pallas_call(kernel, out_shape=(jax.ShapeDtypeStruct((128, 80), BF16),...  13.9 us
    pallas_call x1, Pallas kernels, local(): pl.pallas_call(embed_patches, out_shape=jax.ShapeDtypeStruct((1, 128, HID...  1.88 us

profile of v7, /device:TPU:1, one launch (start us, length us, event | category | flops | bytes accessed | tf_op | source)
XLA Modules:
  0.0 15.8 jit_solution(12267391517756943519)
XLA Ops:
  0.0 13.9 %shard_map.118 = (bf16[128,80]{1,0:T(8,128)(2,1)}, bf16[80,1152]{1,0:T(8,128)(2,1)}) custom-call(s32[1,3]{1,0:T(1,128)} %kind_hbm.1, bf16[1,768,512]{2,1,0:T(8,128)(2,1)} %feat_hbm.1, f32[1,512]{1,0:T(1,128)} %bitcast.8, f32[1,512]{1,0:T(1,128)} %bitcast.9, bf16[4608,512]{1,0:T(8,128)(2,1)} %w_hbm.1, f32[1,512]{1,0:T(1,128)} %bitcast.10, f32[1,512]{1,0:T(1,128)} %bitcast.11, ...), custom_call_target="tpu_custom_call" | custom-call | tf_op jit(solution)/shard_map/pallas_call | solution.py:405
  13.9 1.9 %shard_map.119 = bf16[1,128,1152]{2,1,0:T(8,128)(2,1)} custom-call(bf16[128,80]{1,0:T(8,128)(2,1)} %get-tuple-element.7.patches, bf16[80,1152]{1,0:T(8,128)(2,1)} %get-tuple-element.8.embed), custom_call_target="tpu_custom_call" | custom-call | tf_op jit(solution)/shard_map/pallas_call | solution.py:427

commit v8 on v7

--- a/solution.py
+++ b/solution.py
@@ -153,6 +153,7 @@
 
     col = iota((8, 128), 0)
     lane = iota((8, 128), 1)
+    offset = (lat_bias - LATENT_SHIFT) * LATENT_SCALE
     rows = []
     for r in range(16):
         for h in range(2):
@@ -166,7 +167,7 @@
                 lat = left + pltpu.roll(v, 96, 1) + pltpu.roll(right, 64, 1)
             else:
                 lat = pltpu.roll(left, 32, 1) + v + pltpu.roll(right, 96, 1)
-            lat = (lat + lat_bias - LATENT_SHIFT) * LATENT_SCALE
+            lat = lat * LATENT_SCALE + offset
             rows.append(jnp.where((lane // 16) == (2 * i + col % 2), lat, 0.0))
         if r % 2:
             yield
@@ -358,8 +359,9 @@
     for i in range(N_X):
         pl.when(i != x)(x_arrivals[i].wait_recv)
     rowsum[...] = jnp.sum(xcounts[...], axis=0)
-    exchange([(i > z, z_copies[i], z_ready.at[i]) for i in range(1, N_Z)], False)
+    exchange([((i > z) & (i < 4 + N_Z * jnp.minimum(z, 1)), z_copies[i], z_ready.at[i]) for i in range(1, N_Z)], False)
     convolve(2)
+    exchange([(z == 0, z_copies[i], z_ready.at[i]) for i in range(4, N_Z)], False)
     drain((last(2), 60))
     for i in range(N_DP):
         pl.when(i != rank)(d_arrivals[i].wait_recv)

time: 15.9 us -> 15.3 us (0.962)
  the two profiles are of different devices: /device:TPU:1 before, /device:TPU:224 now
where the time goes in v8:
time: 15.3 us; the launch traced here: 15.2 us
  Pallas kernels  15.2 us (99%)
    pallas_call x1, Pallas kernels, local(): pl.pallas_call(kernel, out_shape=(jax.ShapeDtypeStruct((128, 80), BF16),...  13.4 us
    pallas_call x1, Pallas kernels, local(): pl.pallas_call(embed_patches, out_shape=jax.ShapeDtypeStruct((1, 128, HID...  1.88 us

profile of v8, /device:TPU:224, one launch (start us, length us, event | category | flops | bytes accessed | tf_op | source)
XLA Modules:
  0.0 15.2 jit_solution(12722568994494368225)
XLA Ops:
  0.0 13.4 %shard_map.118 = (bf16[128,80]{1,0:T(8,128)(2,1)}, bf16[80,1152]{1,0:T(8,128)(2,1)}) custom-call(s32[1,3]{1,0:T(1,128)} %kind_hbm.1, bf16[1,768,512]{2,1,0:T(8,128)(2,1)} %feat_hbm.1, f32[1,512]{1,0:T(1,128)} %bitcast.8, f32[1,512]{1,0:T(1,128)} %bitcast.9, bf16[4608,512]{1,0:T(8,128)(2,1)} %w_hbm.1, f32[1,512]{1,0:T(1,128)} %bitcast.10, f32[1,512]{1,0:T(1,128)} %bitcast.11, ...), custom_call_target="tpu_custom_call" | custom-call | tf_op jit(solution)/shard_map/pallas_call | solution.py:407
  13.4 1.9 %shard_map.119 = bf16[1,128,1152]{2,1,0:T(8,128)(2,1)} custom-call(bf16[128,80]{1,0:T(8,128)(2,1)} %get-tuple-element.7.patches, bf16[80,1152]{1,0:T(8,128)(2,1)} %get-tuple-element.8.embed), custom_call_target="tpu_custom_call" | custom-call | tf_op jit(solution)/shard_map/pallas_call | solution.py:429

commit v9 on v8

--- a/solution.py
+++ b/solution.py
@@ -350,10 +350,10 @@
     convolve(0)
     convolve(1)
     exchange([(i > x, x_copies[i], x_ready.at[i]) for i in range(1, N_X)], False)
-    exchange([(i > rank, d_copies[i], d_ready.at[i]) for i in range(1, N_DP)], False)
     drain((last(0), 60), (last(1), 60))
     for t in range(2):
         send_patch(t)
+    exchange([(i > rank, d_copies[i], d_ready.at[i]) for i in range(1, N_DP)], False)
 
     drain((first_norm(2), 42))
     for i in range(N_X):

time: 15.3 us -> 15.5 us (1.013)
  the two profiles are of different devices: /device:TPU:224 before, /device:TPU:17 now
where the time goes in v9:
time: 15.5 us; the launch traced here: 15.4 us
  Pallas kernels  15.4 us (99%)
    pallas_call x1, Pallas kernels, local(): pl.pallas_call(kernel, out_shape=(jax.ShapeDtypeStruct((128, 80), BF16),...  13.6 us
    pallas_call x1, Pallas kernels, local(): pl.pallas_call(embed_patches, out_shape=jax.ShapeDtypeStruct((1, 128, HID...  1.87 us

profile of v9, /device:TPU:17, one launch (start us, length us, event | category | flops | bytes accessed | tf_op | source)
XLA Modules:
  0.0 15.4 jit_solution(1943483784393343288)
XLA Ops:
  0.0 13.6 %shard_map.118 = (bf16[128,80]{1,0:T(8,128)(2,1)}, bf16[80,1152]{1,0:T(8,128)(2,1)}) custom-call(s32[1,3]{1,0:T(1,128)} %kind_hbm.1, bf16[1,768,512]{2,1,0:T(8,128)(2,1)} %feat_hbm.1, f32[1,512]{1,0:T(1,128)} %bitcast.8, f32[1,512]{1,0:T(1,128)} %bitcast.9, bf16[4608,512]{1,0:T(8,128)(2,1)} %w_hbm.1, f32[1,512]{1,0:T(1,128)} %bitcast.10, f32[1,512]{1,0:T(1,128)} %bitcast.11, ...), custom_call_target="tpu_custom_call" | custom-call | tf_op jit(solution)/shard_map/pallas_call | solution.py:407
  13.6 1.9 %shard_map.119 = bf16[1,128,1152]{2,1,0:T(8,128)(2,1)} custom-call(bf16[128,80]{1,0:T(8,128)(2,1)} %get-tuple-element.7.patches, bf16[80,1152]{1,0:T(8,128)(2,1)} %get-tuple-element.8.embed), custom_call_target="tpu_custom_call" | custom-call | tf_op jit(solution)/shard_map/pallas_call | solution.py:429
